TPU v7x, 256 devices: a whole 4x4x8 slice. The times are simulated.
256 devices in a mesh: dp: 2 (over core), ctx: 32 (over z, x), mp: 4 (over y).
Axes of the slice: x: 4, y: 4, z: 8, core: 2. Of those that a mesh axis runs over, the one named last changes fastest.
Arguments:
- image_states: bfloat16 [2, 8192, 8192], P('dp', 'ctx', 'mp'), may hold values from -6 to 6
- place_index: int32 [2, 8192], P('dp'), may hold values from 0 to 16383, as said below
- doc_ids: int32 [2, 16384], P('dp'), may hold values from 0 to 127, never falling along the last dimension, each value on 1 to 512 neighbouring positions
- queries: bfloat16 [2, 16384, 4096], P('dp', 'ctx', 'mp'), may hold values from -160 to 160
- text_kv: bfloat16 [2, 16384, 1024], P('dp', 'ctx', 'mp'), may hold values from -5.5 to 5.5
- kv_weight: bfloat16 [4, 8192, 256], P('mp'), may hold values from -0.0625 to 0.0625
- d_out: bfloat16 [2, 16384, 4096], P('dp', 'ctx', 'mp'), may hold values from -6 to 6
Outputs:
- attn_out: bfloat16 [2, 16384, 4096], P('dp', 'ctx', 'mp')
- image_grad: bfloat16 [2, 8192, 8192], P('dp', 'ctx', 'mp')
- kv_weight_grad: float32 [4, 8192, 256], P('mp', 'ctx')
Inputs may be any that keep to these rules, and one draw needn't show every extreme that they name: `place_index`: images are whole blocks of 16 image tokens, consecutive in a vision rank's order and placed on 16 consecutive positions aligned to 16; every context shard of 512 positions holds exactly 256 image tokens; no position gets two image tokens; at most 16 image tokens of one vision rank lie in one context shard, and in every draw some vision rank places exactly 16 in some shard.
All inputs are finite; a program needn't handle non-finite values.
Results may differ from a plain program's by a relative error of at most 0.0085.
Values may be sent and summed in bfloat16 or wider, within the bound.
A program may use at most 128 MiB of HBM per device.

v0:
```python
import jax
import jax.numpy as jnp
from jax import lax
from jax.sharding import PartitionSpec as P

IMGTOK = 16


def shifted_2(block, axis, distance):
    devices = range(lax.axis_size(axis))
    route = [(i - distance, i) for i in devices if i - distance in devices]
    return lax.ppermute(block, axis, route)


def routing_tables(place_row, shard_index, image_dev, capacity, ctx_dev, rank_count):
    dest_shard = place_row // ctx_dev
    by_source = dest_shard.reshape(rank_count, image_dev)
    onehot = (
        by_source[:, :, None] == jnp.arange(rank_count, dtype=jnp.int32)[None, None, :]
    ).astype(jnp.int32)
    running = jnp.cumsum(onehot, axis=1) - 1
    slot_index = jnp.sum(running * onehot, axis=2).reshape(-1)
    source_rank = jnp.arange(rank_count * image_dev, dtype=jnp.int32) // image_dev
    send_flat = dest_shard * capacity + slot_index
    recv_flat = source_rank * capacity + slot_index
    is_mine = dest_shard == shard_index
    local_pos = place_row % ctx_dev
    image_marks = (
        jnp.zeros((ctx_dev,), jnp.int32)
        .at[jnp.where(is_mine, local_pos, ctx_dev)]
        .set(1, mode="drop")
    )
    compact_of_pos = jnp.cumsum(image_marks) - 1
    compact = jnp.where(is_mine, compact_of_pos[local_pos], image_dev)
    recv_of_compact = jnp.zeros((image_dev,), jnp.int32).at[compact].set(recv_flat, mode="drop")
    image_pos = jnp.nonzero(image_marks, size=image_dev)[0].astype(jnp.int32)
    own_slots = lax.dynamic_slice_in_dim(send_flat, shard_index * image_dev, image_dev)
    return (own_slots, recv_of_compact, image_pos)


def per_device(image_states, place_index, doc_ids, queries, text_kv, kv_weight, d_out):
    rank_count = lax.axis_size("ctx")
    shard_index = lax.axis_index("ctx")
    ctx_dev = queries.shape[1]
    image_dev = image_states.shape[1]
    head_size = kv_weight.shape[2] // 2
    group_size = queries.shape[2] // head_size
    capacity = IMGTOK * ((image_dev // IMGTOK + rank_count - 1) // rank_count)
    own_slots, recv_of_compact, image_pos = routing_tables(
        place_index[0], shard_index, image_dev, capacity, ctx_dev, rank_count
    )
    weights = kv_weight[0]
    own_states = image_states[0]
    holder = (
        jnp.zeros((rank_count * capacity, own_states.shape[1]), own_states.dtype)
        .at[own_slots]
        .set(own_states)
    )
    arrived = lax.all_to_all(
        holder.reshape(rank_count, capacity, own_states.shape[1]),
        "ctx",
        split_axis=0,
        concat_axis=0,
        tiled=True,
    )
    state_rows = lax.all_gather(
        arrived.reshape(rank_count * capacity, arrived.shape[2])[recv_of_compact],
        "mp",
        axis=1,
        tiled=True,
    )
    image_kv = jnp.dot(state_rows, weights, preferred_element_type=jnp.float32).astype(jnp.bfloat16)
    kv_local = text_kv[0].at[image_pos].set(image_kv)
    earlier = shifted_2(kv_local, "ctx", 1)
    key_window = jnp.concatenate([earlier, kv_local], axis=0)
    key_part = key_window[:, :head_size]
    value_part = key_window[:, head_size:]
    all_docs = doc_ids[0]
    own_docs = lax.dynamic_slice_in_dim(all_docs, shard_index * ctx_dev, ctx_dev)
    prior_docs = lax.dynamic_slice_in_dim(
        all_docs, jnp.maximum(shard_index - 1, 0) * ctx_dev, ctx_dev
    )
    prior_docs = jnp.where(shard_index > 0, prior_docs, -1)
    key_docs = jnp.concatenate([prior_docs, own_docs], axis=0)
    query_pos = jnp.arange(ctx_dev, dtype=jnp.int32)
    key_pos = jnp.arange(2 * ctx_dev, dtype=jnp.int32) - ctx_dev
    allowed = (key_pos[None, :] <= query_pos[:, None]) & (key_docs[None, :] == own_docs[:, None])
    score_scale = head_size ** (-0.5)
    query_heads = queries[0].reshape(ctx_dev, group_size, head_size).transpose(1, 0, 2)
    grad_heads = d_out[0].reshape(ctx_dev, group_size, head_size).transpose(1, 0, 2)

    def one_head(running_sums, head_inputs):
        query_head, grad_head = head_inputs
        scores = (
            lax.dot_general(
                query_head, key_part, (((1,), (1,)), ((), ())), preferred_element_type=jnp.float32
            )
            * score_scale
        )
        scores = jnp.where(allowed, scores, -1e30)
        shifted = jnp.exp(scores - jnp.max(scores, axis=1, keepdims=True))
        shifted = jnp.where(allowed, shifted, 0.0)
        attention = shifted / jnp.sum(shifted, axis=1, keepdims=True)
        attention_low = attention.astype(jnp.bfloat16)
        context = jnp.dot(attention_low, value_part, preferred_element_type=jnp.float32)
        grad_attention = lax.dot_general(
            grad_head, value_part, (((1,), (1,)), ((), ())), preferred_element_type=jnp.float32
        )
        row_delta = jnp.sum(grad_head.astype(jnp.float32) * context, axis=1, keepdims=True)
        grad_scores = (attention * (grad_attention - row_delta)).astype(jnp.bfloat16)
        key_grad = running_sums[0] + score_scale * lax.dot_general(
            grad_scores, query_head, (((0,), (0,)), ((), ())), preferred_element_type=jnp.float32
        )
        value_grad = running_sums[1] + lax.dot_general(
            attention_low, grad_head, (((0,), (0,)), ((), ())), preferred_element_type=jnp.float32
        )
        return ((key_grad, value_grad), context.astype(jnp.bfloat16))

    zero_grads = jnp.zeros((2 * ctx_dev, head_size), jnp.float32)
    (key_grad, value_grad), outputs = lax.scan(
        one_head, (zero_grads, zero_grads), (query_heads, grad_heads)
    )
    attn_out = outputs.transpose(1, 0, 2).reshape(ctx_dev, group_size * head_size)
    kv_grad = jnp.concatenate([key_grad, value_grad], axis=1)
    later = shifted_2(kv_grad[:ctx_dev], "ctx", -1)
    total_grad = kv_grad[ctx_dev:] + later
    grad_low = total_grad[image_pos].astype(jnp.bfloat16)
    partial_value = lax.dot_general(
        grad_low, weights, (((1,), (1,)), ((), ())), preferred_element_type=jnp.float32
    )
    grad_rows = lax.psum_scatter(partial_value, "mp", scatter_dimension=1, tiled=True).astype(
        jnp.bfloat16
    )
    holder = (
        jnp.zeros((rank_count * capacity, grad_rows.shape[1]), grad_rows.dtype)
        .at[recv_of_compact]
        .set(grad_rows)
    )
    back = lax.all_to_all(
        holder.reshape(rank_count, capacity, grad_rows.shape[1]),
        "ctx",
        split_axis=0,
        concat_axis=0,
        tiled=True,
    )
    image_grad = back.reshape(rank_count * capacity, back.shape[2])[own_slots]
    weight_share = lax.psum_scatter(
        lax.dot_general(
            state_rows, grad_low, (((0,), (0,)), ((), ())), preferred_element_type=jnp.float32
        ),
        "ctx",
        scatter_dimension=0,
        tiled=True,
    )
    weight_grad = lax.psum(weight_share, "dp")
    return (attn_out[None], image_grad[None], weight_grad[None])


def solution(mesh):
    in_specs = (
        P("dp", "ctx", "mp"),
        P("dp", None),
        P("dp", None),
        P("dp", "ctx", "mp"),
        P("dp", "ctx", "mp"),
        P("mp", None, None),
        P("dp", "ctx", "mp"),
    )
    out_specs = (P("dp", "ctx", "mp"), P("dp", "ctx", "mp"), P("mp", "ctx", None))
    return jax.shard_map(
        per_device, mesh=mesh, in_specs=in_specs, out_specs=out_specs, check_vma=False
    )
```

profile of v0, /device:TPU:17, one launch (start us, length us, event | category | flops | bytes accessed | tf_op | source)
XLA Modules:
  0.0 720.2 jit_solution(6062487333594903652)
XLA Ops:
  9.8 18.4 %reduce-window.39 = s32[32,32,2,128]{3,1,2,0:T(8,128)S(1)} reduce-window(s32[32,32,2,128]{3,1,2,0:T(8,128)S(1)} %fusion.43, s32[]{:T(128)} %constant.112.clone.1), window={size=1x1x1x128 pad=0_0x0_0x0_0x127_0}, to_apply=%region_7.8 | reduce-window | flops 33292288 | bytes 2097156 | tf_op jit(solution)/shard_map/reduce-window.4
  31.0 3.7 scatter_custom_fusion.2
  34.8 11.0 %all-to-all-start = ((bf16[32,16,2048]{2,1,0:T(8,128)(2,1)}), bf16[32,16,2048]{2,1,0:T(8,128)(2,1)S(1)}, u32[]{:S(2)}, u32[]{:S(2)}) async-start(bf16[32,16,2048]{2,1,0:T(8,128)(2,1)} %bitcast.124), calls=%async_computation | async-start | bytes 4194304 | tf_op jit(solution)/shard_map/all_to_all | solution.py:59
  46.3 30.4 %scatter_custom_fusion = s32[512]{0:T(512)S(1)} fusion(s32[8192]{0:T(1024)S(1)} %bitcast.141, s32[8192]{0:T(1024)S(1)} %broadcast.432, s32[]{:T(128)} %constant.112.clone.1), kind=kCustom, calls=%fused_computation.133 | custom fusion | bytes 2052 | tf_op jit(solution)/shard_map/scatter | solution.py:31
  77.3 51.2 %gather_fusion = s32[8192]{0:T(1024)S(1)} fusion(s32[512]{0:T(512)S(1)} %add_bitcast_fusion.1, s32[8192]{0:T(1024)S(1)} %broadcast_clamp_fusion), kind=kCustom, calls=%fused_computation | custom fusion | bytes 98304 | tf_op jit(solution)/shard_map/gather | solution.py:34
  128.6 30.4 %scatter_custom_fusion.3 = s32[256]{0:T(256)S(1)} fusion(s32[8192]{0:T(1024)S(1)} %bitcast.140, s32[8192]{0:T(1024)S(1)} %fusion.49, s32[]{:T(128)} %constant.112.clone.1), kind=kCustom, calls=%fused_computation.136 | custom fusion | bytes 1028 | tf_op jit(solution)/shard_map/scatter | solution.py:35
  159.1 2.3 gather_fusion.1
  162.8 4.1 scatter_custom_fusion.1
  168.1 44.7 %all-gather.3.cloned.1.call-done = bf16[256,8192]{1,0:T(8,128)(2,1)} async-done(((bf16[256,2048]{1,0:T(8,128)(2,1)}), bf16[256,8192]{1,0:T(8,128)(2,1)}) %all-gather.3.cloned.1.call-update) | async-done | bytes 4194320 | tf_op jit(solution)/shard_map/all_gather | solution.py:66
  212.8 4.7 fusion.32
  217.6 1.8 scatter_fusion
  219.4 3.8 collective-permute-start
  229.0 86.4 %while.15 = (s32[]{:T(128)}, f32[1024,128]{1,0:T(8,128)}, f32[1024,128]{1,0:T(8,128)}, bf16[8,512,128]{1,2,0:T(8,128)(2,1)}, bf16[8,512,128]{1,2,0:T(8,128)(2,1)...) while((s32[]{:T(128)}, f32[1024,128]{1,0:T(8,128)}, ...), condition=%wide.region_19.20_spmd.clone, body=%wide.region_15.19_spmd.clone.sunk | while | flops 686160384 | bytes 18659980 | solution.py:120
  229.0 1.8 fusion.93
  234.7 2.6 fusion.96
  237.3 2.2 convolution_add_fusion.2
  239.5 1.8 fusion.93
  245.2 2.8 fusion.96
  247.9 2.4 convolution_add_fusion.2
  250.3 1.8 fusion.93
  256.0 2.8 fusion.96
  258.8 2.4 convolution_add_fusion.2
  261.2 1.8 fusion.93
  266.9 2.8 fusion.96
  269.6 2.4 convolution_add_fusion.2
  272.0 1.8 fusion.93
  277.7 2.8 fusion.96
  280.5 2.4 convolution_add_fusion.2
  282.9 1.8 fusion.93
  288.6 2.8 fusion.96
  291.3 2.4 convolution_add_fusion.2
  293.7 1.8 fusion.93
  299.4 2.8 fusion.96
  302.2 2.4 convolution_add_fusion.2
  304.6 1.8 fusion.93
  310.3 2.8 fusion.96
  313.0 2.4 convolution_add_fusion.2
  319.0 13.5 %collective-permute-done.1 = f32[512,256]{1,0:T(8,128)S(1)} collective-permute-done((f32[512,256]{1,0:T(8,128)S(1)}, f32[512,256]{1,0:T(8,128)S(1)}, u32[]{:S(2)}, u32[]{:S(2)}) %collective-permute-start.1) | collective-permute-done | bytes 524320 | tf_op jit(solution)/shard_map/ppermute | solution.py:12
  333.7 6.7 fusion.28
  340.4 6.7 fusion.67
  347.2 79.8 %reduce-scatter.3.cloned.1.call-done = f32[256,2048]{1,0:T(8,128)} async-done(((f32[256,8192]{1,0:T(8,128)}), f32[256,2048]{1,0:T(8,128)}) %reduce-scatter.3.cloned.1.call-update) | async-done | bytes 2097168 | tf_op jit(solution)/shard_map/reduce_scatter | solution.py:131
  427.0 4.8 scatter_custom_fusion.5
  431.9 9.5 %all-to-all-start.1 = ((bf16[32,16,2048]{2,1,0:T(8,128)(2,1)}), bf16[32,16,2048]{2,1,0:T(8,128)(2,1)S(1)}, u32[]{:S(2)}, u32[]{:S(2)}) async-start(bf16[32,16,2048]{2,1,0:T(8,128)(2,1)} %bitcast.125), calls=%async_computation.2 | async-start | bytes 4194304 | tf_op jit(solution)/shard_map/all_to_all | solution.py:139
  441.5 236.1 %reduce-scatter.5.cloned.1.call-done = f32[256,256]{1,0:T(8,128)} async-done(((f32[8192,256]{1,0:T(8,128)}), f32[256,256]{1,0:T(8,128)}) %reduce-scatter.5.cloned.1.call-update) | async-done | bytes 262160 | tf_op jit(solution)/shard_map/reduce_scatter | solution.py:147
  677.6 2.3 copy.19
  679.9 2.3 gather_fusion.3
  682.2 29.8 %all-reduce.2.cloned.1.call-done = f32[1,256,256]{2,1,0:T(8,128)} async-done(((f32[1,256,256]{2,1,0:T(8,128)}), f32[1,256,256]{2,1,0:T(8,128)}) %all-reduce.2.cloned.1.call-update) | async-done | bytes 262160 | tf_op jit(solution)/shard_map/psum | solution.py:155
  712.0 1.7 copy.43
  (115 shorter events, 50.6 us)
Async XLA Ops:
  7.2 23.9 %copy-start = (bf16[1,256,2048]{2,1,0:T(8,128)(2,1)S(1)}, bf16[1,256,2048]{2,1,0:T(8,128)(2,1)}, u32[]{:S(2)}) copy-start(bf16[1,256,2048]{2,1,0:T(8,128)(2,1)} %param.9) | copy-start | bytes 3145732
  28.2 1.4 copy-start.2
  34.8 124.3 %all-to-all-start = ((bf16[32,16,2048]{2,1,0:T(8,128)(2,1)}), bf16[32,16,2048]{2,1,0:T(8,128)(2,1)S(1)}, u32[]{:S(2)}, u32[]{:S(2)}) async-start(bf16[32,16,2048]{2,1,0:T(8,128)(2,1)} %bitcast.124), calls=%async_computation | async-start | bytes 4194304 | tf_op jit(solution)/shard_map/all_to_all | solution.py:59
  45.8 167.0 %all-gather.3.cloned.1.call-start = ((), (), s32[]{:S(2)}) async-start(), calls=%async_computation.7 | async-start | bytes 5242880 | tf_op jit(solution)/shard_map/all_gather | solution.py:66
  161.5 265.6 %reduce-scatter.3.cloned.1.call-start = ((), (), s32[]{:S(2)}) async-start(), calls=%async_computation.4 | async-start | bytes 10485760 | tf_op jit(solution)/shard_map/reduce_scatter | solution.py:131
  168.1 49.4 %copy-start.1 = (bf16[1,512,256]{2,1,0:T(8,128)(2,1)S(1)}, bf16[1,512,256]{2,1,0:T(8,128)(2,1)}, u32[]{:S(2)}) copy-start(bf16[1,512,256]{2,1,0:T(8,128)(2,1)} %param.13) | copy-start | bytes 786436
  217.5 5.7 copy-start.3
  217.6 7.0 copy-start.4
  219.4 7.9 %collective-permute-start = (bf16[512,256]{1,0:T(8,128)(2,1)S(1)}, bf16[512,256]{1,0:T(8,128)(2,1)}, u32[]{:S(2)}, u32[]{:S(2)}) collective-permute-start(bf16[512,256]{1,0:T(8,128)(2,1)S(1)} %scatter_fusion), channel_id=1, source_target_pairs={{0,4},{4,8},{8,12},{12,16},{16,20},{20,24},{24,28},{28,32},{32,36}... | collective-permute-start | bytes 786440 | tf_op jit(solution)/shard_map/ppermute | solution.py:12
  317.7 14.8 %collective-permute-start.1 = (f32[512,256]{1,0:T(8,128)S(1)}, f32[512,256]{1,0:T(8,128)S(1)}, u32[]{:S(2)}, u32[]{:S(2)}) collective-permute-start(f32[512,256]{1,0:T(8,128)S(1)} %slice.64), channel_id=1, source_target_pairs={{4,0},{8,4},{12,8},{16,12},{20,16},{24,20},{28,24},{32,28},{36,32}... | collective-permute-start | bytes 1572872 | tf_op jit(solution)/shard_map/ppermute | solution.py:12
  340.4 337.2 %reduce-scatter.5.cloned.1.call-start = ((), (), s32[]{:S(2)}) async-start(), calls=%async_computation.5 | async-start | bytes 8650752 | tf_op jit(solution)/shard_map/reduce_scatter | solution.py:147
  431.9 248.0 %all-to-all-start.1 = ((bf16[32,16,2048]{2,1,0:T(8,128)(2,1)}), bf16[32,16,2048]{2,1,0:T(8,128)(2,1)S(1)}, u32[]{:S(2)}, u32[]{:S(2)}) async-start(bf16[32,16,2048]{2,1,0:T(8,128)(2,1)} %bitcast.125), calls=%async_computation.2 | async-start | bytes 4194304 | tf_op jit(solution)/shard_map/all_to_all | solution.py:139
  441.4 270.6 %all-reduce.2.cloned.1.call-start = ((), (), s32[]{:S(2)}) async-start(), calls=%async_computation.6 | async-start | bytes 524288 | tf_op jit(solution)/shard_map/psum | solution.py:155
Sparse Core Ops, SparseCore 0:
  161.6 51.1 all-gather.2
  340.5 86.4 reduce-scatter.2
  431.1 246.4 reduce-scatter.4
  680.0 31.9 all-reduce.1
where the time goes:
time: 723 us; the launch traced here: 720 us
  waiting for transfers between devices  405 us (56%)
  local copies, waits for them, and re-layouts  141 us (20%)
  matrix products  84.7 us (12%)
  other arithmetic  49.5 us (7%)
  starting transfers between devices  25.9 us (4%)
  between operations  14.1 us (2%)
    reduce_scatter x1, waiting for transfers between devices, per_device(): lax.psum_scatter(lax.dot_general(state_rows, grad_low, (((0,), (0,)), (()...  236 us
    reduce_scatter x1, waiting for transfers between devices, per_device(): lax.psum_scatter(partial_value, 'mp', scatter_dimension=1, tiled=True)  79.8 us
    gather x1, local copies, waits for them, and re-layouts, routing_tables(): compact = jnp.where(is_mine, compact_of_pos[local_pos], image_dev)  51.2 us
    all_gather x1, waiting for transfers between devices, per_device(): lax.all_gather(arrived.reshape(rank_count * capacity, arrived.shape[2])[r...  44.7 us
    scatter x1, local copies, waits for them, and re-layouts, routing_tables(): image_marks = jnp.zeros((ctx_dev,), jnp.int32).at[jnp.where(is_mine, loca...  30.4 us
    scatter x1, local copies, waits for them, and re-layouts, routing_tables(): jnp.zeros((image_dev,), jnp.int32).at[compact].set(recv_flat, mode='drop')  30.4 us
    psum x1, waiting for transfers between devices, per_device(): weight_grad = lax.psum(weight_share, 'dp')  29.8 us
    dot_general x8, matrix products, one_head(): lax.dot_general(grad_scores, query_head, (((0,), (0,)), ((), ())), prefer...  21.9 us
  transfers between devices with their start and end apart: 8, of which 6 were waited for; matrix products, arithmetic and copies ran while one was open for 19% of the time, Pallas kernels for 0%

commit v1 on v0

v1 whole, which is shorter than its diff:
```python
import functools
import math

import jax
import jax.numpy as jnp
from jax import lax
from jax.experimental import pallas as pl
from jax.experimental.pallas import tpu as pltpu
from jax.sharding import PartitionSpec as P

IMGTOK = 16
BF16 = jnp.bfloat16
F32 = jnp.float32
MESH = pl.DeviceIdType.MESH


def dot_nn(a, b):
    return jnp.dot(a, b, preferred_element_type=F32)


def dot_nt(a, b):
    return lax.dot_general(a, b, (((1,), (1,)), ((), ())), preferred_element_type=F32)


def iota(shape, dim):
    return lax.broadcasted_iota(jnp.int32, shape, dim)


def ring_order(count):
    return sorted(range(count), key=lambda k: (min(k, count - k), k))


def remote(src, dst, send_sem, recv_sem, device):
    return pltpu.make_async_remote_copy(
        src_ref=src,
        dst_ref=dst,
        send_sem=send_sem,
        recv_sem=recv_sem,
        device_id=device,
        device_id_type=MESH,
    )


def slot_exchange(packed, arrived, send_sems, recv_sems, c, n):
    def copy_of(k):
        p = lax.rem(c + k, n)
        return remote(
            packed.at[pl.ds(pl.multiple_of(p * IMGTOK, IMGTOK), IMGTOK)],
            arrived.at[pl.ds(pl.multiple_of(c * IMGTOK, IMGTOK), IMGTOK)],
            send_sems.at[k],
            recv_sems.at[k],
            {"ctx": p},
        )

    def start(k, carry):
        copy_of(k).start()
        return carry

    def finish(k, carry):
        copy_of(k).wait()
        return carry

    lax.fori_loop(1, n, start, 0)
    mine = pl.ds(pl.multiple_of(c * IMGTOK, IMGTOK), IMGTOK)
    arrived[mine, :] = packed[mine, :]
    lax.fori_loop(1, n, finish, 0)


def route_kernel(
    n,
    mp,
    slot_row,
    pos_row,
    text,
    states,
    weights,
    own_out,
    prev_out,
    wh_out,
    sht_out,
    sh,
    wh,
    sht,
    psend,
    precv,
    acc,
    yrecv,
    packed,
    arrived,
    own_kv,
    prev_kv,
    local_sems,
    s_sems,
    w_send,
    w_recv,
    p_send,
    p_recv,
    y_send,
    y_recv,
    a_send,
    a_recv,
    k_sems,
):
    c = lax.axis_index("ctx")
    m = lax.axis_index("mp")
    d = lax.axis_index("dp")
    half = sh.shape[2]
    tokens = sh.shape[1]
    order = ring_order(mp)

    get_w = pltpu.make_async_copy(
        weights.at[pl.ds(pl.multiple_of(m * 2 * half + d * half, half), half)],
        wh.at[m],
        local_sems.at[0],
    )
    get_s = pltpu.make_async_copy(
        states.at[:, pl.ds(pl.multiple_of(d * half, half), half)], sh.at[d], local_sems.at[1]
    )
    get_w.start()
    get_s.start()

    barrier = pltpu.get_barrier_semaphore()
    pl.semaphore_signal(barrier, inc=1, device_id={"dp": 1 - d}, device_id_type=MESH)
    for k in range(1, mp):
        pl.semaphore_signal(
            barrier, inc=1, device_id={"mp": lax.rem(m + k, mp)}, device_id_type=MESH
        )

    def greet(k, carry):
        pl.semaphore_signal(
            barrier, inc=1, device_id={"ctx": lax.rem(c + k, n)}, device_id_type=MESH
        )
        return carry

    lax.fori_loop(1, n, greet, 0)
    pl.semaphore_wait(barrier, 1 + (mp - 1) + (n - 1))

    w_copies = {}
    for k in reversed(order):
        if k:
            p = lax.rem(m + k, mp)
            w_copies[k] = remote(
                weights.at[pl.ds(pl.multiple_of(p * 2 * half + d * half, half), half)],
                wh.at[m],
                w_send.at[k],
                w_recv.at[k],
                {"mp": p},
            )
            w_copies[k].start()
    s_copy = remote(
        states.at[:, pl.ds(pl.multiple_of((1 - d) * half, half), half)],
        sh.at[d],
        s_sems.at[0],
        s_sems.at[1],
        {"dp": 1 - d},
    )
    s_copy.start()
    get_s.wait()
    get_w.wait()
    s_copy.wait()
    for b in range(2):
        sht[:, b * tokens : (b + 1) * tokens] = sh[b].T
    put_sht = pltpu.make_async_copy(sht, sht_out, local_sems.at[2])
    put_sht.start()

    p_copies = {}
    for k in order:
        h = lax.rem(m - k + mp, mp)
        if k:
            w_copies[k].wait_recv()
        psend[k] = dot_nn(sh[1 - d], wh[h])
        p_copies[k] = remote(
            psend.at[k], precv.at[k], p_send.at[k], p_recv.at[k], {"dp": 1 - d}
        )
        p_copies[k].start()
        acc[k] = dot_nn(sh[d], wh[h])
    put_wh = pltpu.make_async_copy(wh, wh_out, local_sems.at[3])
    put_wh.start()

    y_copies = {}
    for k in reversed(order):
        p_copies[k].wait_recv()
        acc[k] = acc[k] + precv[k]
        if k:
            y_copies[k] = remote(
                acc.at[k],
                yrecv.at[k],
                y_send.at[k],
                y_recv.at[k],
                {"mp": lax.rem(m - k + mp, mp)},
            )
            y_copies[k].start()
    total = acc[0]
    for k in order:
        if k:
            y_copies[k].wait_recv()
            total = total + yrecv[k]
    image_kv = total.astype(BF16)

    pick = (iota((n * IMGTOK, tokens), 0) == slot_row[...]).astype(F32).astype(BF16)
    packed[...] = dot_nn(pick, image_kv).astype(BF16)
    slot_exchange(packed, arrived, a_send, a_recv, c, n)

    place = (iota((text.shape[0], n * IMGTOK), 0) == pos_row[...]).astype(F32)
    is_image = jnp.sum(place, axis=1, keepdims=True) > 0.5
    placed = dot_nn(place.astype(BF16), arrived[...])
    own_kv[...] = jnp.where(is_image, placed, text[...].astype(F32)).astype(BF16)
    shift = remote(
        own_kv, prev_kv, k_sems.at[0], k_sems.at[1], {"ctx": lax.rem(c + 1, n)}
    )
    shift.start()
    put_own = pltpu.make_async_copy(own_kv, own_out, local_sems.at[4])
    put_own.start()
    shift.wait()
    put_prev = pltpu.make_async_copy(prev_kv, prev_out, local_sems.at[5])
    put_prev.start()

    for k in range(mp):
        p_copies[k].wait_send()
        if k:
            w_copies[k].wait_send()
            y_copies[k].wait_send()
    put_sht.wait()
    put_wh.wait()
    put_own.wait()
    put_prev.wait()


def route(slot_row, pos_row, text, states, weights, n, mp):
    tokens, slice_width = states.shape
    half = slice_width // 2
    width = weights.shape[1]
    ctx_dev = text.shape[0]
    slots = n * IMGTOK
    vmem = pl.BlockSpec(memory_space=pltpu.VMEM)
    hbm = pl.BlockSpec(memory_space=pl.ANY)
    dma = pltpu.SemaphoreType.DMA
    return pl.pallas_call(
        functools.partial(route_kernel, n, mp),
        out_shape=(
            jax.ShapeDtypeStruct((ctx_dev, width), BF16),
            jax.ShapeDtypeStruct((ctx_dev, width), BF16),
            jax.ShapeDtypeStruct((mp, half, width), BF16),
            jax.ShapeDtypeStruct((half, 2 * tokens), BF16),
        ),
        in_specs=[vmem, vmem, vmem, hbm, hbm],
        out_specs=(hbm, hbm, hbm, hbm),
        scratch_shapes=[
            pltpu.VMEM((2, tokens, half), BF16),
            pltpu.VMEM((mp, half, width), BF16),
            pltpu.VMEM((half, 2 * tokens), BF16),
            pltpu.VMEM((mp, tokens, width), F32),
            pltpu.VMEM((mp, tokens, width), F32),
            pltpu.VMEM((mp, tokens, width), F32),
            pltpu.VMEM((mp, tokens, width), F32),
            pltpu.VMEM((slots, width), BF16),
            pltpu.VMEM((slots, width), BF16),
            pltpu.VMEM((ctx_dev, width), BF16),
            pltpu.VMEM((ctx_dev, width), BF16),
            dma((6,)),
            dma((2,)),
            dma((mp,)),
            dma((mp,)),
            dma((mp,)),
            dma((mp,)),
            dma((mp,)),
            dma((mp,)),
            dma((n,)),
            dma((n,)),
            dma((2,)),
        ],
        compiler_params=pltpu.CompilerParams(
            collective_id=0, has_side_effects=True, vmem_limit_bytes=40 << 20
        ),
        name="route",
    )(slot_row, pos_row, text, states, weights)


def attention_kernel(
    block,
    q_docs,
    k_docs,
    q_ref,
    g_ref,
    prev,
    own,
    out,
    prev_grad,
    own_grad,
    bias,
    keys,
    vals,
    vals_t,
    key_sum,
    val_sum,
):
    step = pl.program_id(0)
    size, hd = q_ref.shape
    span = size + block
    scale = hd ** (-0.5)
    to_log2 = scale / math.log(2.0)

    @pl.when(step == 0)
    def _():
        keys[:size] = prev[:, :hd]
        keys[size:] = own[:, :hd]
        vals[:size] = prev[:, hd:]
        vals[size:] = own[:, hd:]
        vals_t[...] = vals[...].T
        key_sum[...] = jnp.zeros_like(key_sum)
        val_sum[...] = jnp.zeros_like(val_sum)
        for i in range(size // block):
            first = i * block
            key_pos = iota((span, block), 0) + (first - size)
            query_pos = iota((span, block), 1) + first
            allowed = (key_pos <= query_pos) & (
                k_docs[first : first + span, :] == q_docs[:, first : first + block]
            )
            bias[i] = jnp.where(allowed, 0.0, -1e30)

    for i in range(size // block):
        first = i * block
        rows = slice(first, first + block)
        window = slice(first, first + span)
        q = q_ref[rows, :]
        g = g_ref[rows, :]
        scores = dot_nt(keys[window, :], q) * to_log2 + bias[i]
        shifted = jnp.exp2(scores - jnp.max(scores, axis=0, keepdims=True))
        probs = shifted * (1.0 / jnp.sum(shifted, axis=0, keepdims=True))
        low = probs.astype(BF16)
        context = dot_nn(vals_t[:, window], low)
        grad_probs = dot_nt(vals[window, :], g)
        delta = jnp.sum(g.T.astype(F32) * context, axis=0, keepdims=True)
        grad_scores = (probs * (grad_probs - delta)).astype(BF16)
        out[rows, :] = context.T.astype(BF16)
        key_sum[window, :] += dot_nn(grad_scores, q)
        val_sum[window, :] += dot_nn(low, g)

    @pl.when(step == pl.num_programs(0) - 1)
    def _():
        prev_grad[:, :hd] = (key_sum[:size] * scale).astype(BF16)
        prev_grad[:, hd:] = val_sum[:size].astype(BF16)
        own_grad[:, :hd] = key_sum[size:] * scale
        own_grad[:, hd:] = val_sum[size:]


def attention(q_docs, k_docs, queries, grads, prev, own, hd):
    size, width = queries.shape
    block = size // 2
    fixed = lambda g: (0, 0)
    by_head = lambda g: (0, g)
    return pl.pallas_call(
        functools.partial(attention_kernel, block),
        grid=(width // hd,),
        out_shape=(
            jax.ShapeDtypeStruct((size, width), BF16),
            jax.ShapeDtypeStruct((size, 2 * hd), BF16),
            jax.ShapeDtypeStruct((size, 2 * hd), F32),
        ),
        in_specs=[
            pl.BlockSpec((1, size), fixed),
            pl.BlockSpec((2 * size, 1), fixed),
            pl.BlockSpec((size, hd), by_head),
            pl.BlockSpec((size, hd), by_head),
            pl.BlockSpec((size, 2 * hd), fixed),
            pl.BlockSpec((size, 2 * hd), fixed),
        ],
        out_specs=(
            pl.BlockSpec((size, hd), by_head),
            pl.BlockSpec((size, 2 * hd), fixed),
            pl.BlockSpec((size, 2 * hd), fixed),
        ),
        scratch_shapes=[
            pltpu.VMEM((2, size + block, block), F32),
            pltpu.VMEM((2 * size, hd), BF16),
            pltpu.VMEM((2 * size, hd), BF16),
            pltpu.VMEM((hd, 2 * size), BF16),
            pltpu.VMEM((2 * size, hd), F32),
            pltpu.VMEM((2 * size, hd), F32),
        ],
        compiler_params=pltpu.CompilerParams(
            dimension_semantics=("arbitrary",), vmem_limit_bytes=48 << 20
        ),
        name="attention",
    )(q_docs, k_docs, queries, grads, prev, own)


def grad_kernel(
    n,
    mp,
    nx,
    nz,
    pos_col,
    slot_col,
    prev_grad,
    own_grad,
    wh,
    sht,
    image_out,
    weight_out,
    later,
    packed,
    arrived,
    gall,
    xs,
    xr,
    ys,
    yr,
    zr,
    wg_send,
    wg_recv,
    ig_send,
    ig_recv,
    k_sems,
    a_send,
    a_recv,
    f_send,
    f_recv,
    g_send,
    g_recv,
    x_send,
    x_recv,
    y_send,
    y_recv,
    z_send,
    z_recv,
    o_sems,
):
    c = lax.axis_index("ctx")
    m = lax.axis_index("mp")
    d = lax.axis_index("dp")
    z = c // nx
    x = lax.rem(c, nx)
    order = ring_order(mp)
    size = own_grad.shape[0]
    tokens = slot_col.shape[0]
    half = wh.shape[1]
    chunk = half // nx
    part = chunk // 2
    slots = n * IMGTOK

    barrier = pltpu.get_barrier_semaphore()
    pl.semaphore_signal(barrier, inc=1, device_id={"dp": 1 - d}, device_id_type=MESH)
    for k in range(1, mp):
        pl.semaphore_signal(
            barrier, inc=1, device_id={"mp": lax.rem(m + k, mp)}, device_id_type=MESH
        )

    def greet(k, carry):
        pl.semaphore_signal(
            barrier, inc=1, device_id={"ctx": lax.rem(c + k, n)}, device_id_type=MESH
        )
        return carry

    def greet_other(k, carry):
        pl.semaphore_signal(
            barrier,
            inc=1,
            device_id={"dp": 1 - d, "ctx": lax.rem(z + k, nz) * nx + x},
            device_id_type=MESH,
        )
        return carry

    lax.fori_loop(1, n, greet, 0)
    lax.fori_loop(1, nz, greet_other, 0)
    pl.semaphore_wait(barrier, 1 + (mp - 1) + (n - 1) + (nz - 1))

    shift = remote(
        prev_grad, later, k_sems.at[0], k_sems.at[1], {"ctx": lax.rem(c + n - 1, n)}
    )
    shift.start()
    spread = (pos_col[...] == iota((slots, size), 1)).astype(F32).astype(BF16)
    collect = (slot_col[...] == iota((tokens, slots), 1)).astype(F32).astype(BF16)
    shift.wait()
    grad_low = (own_grad[...] + later[...].astype(F32)).astype(BF16)
    packed[...] = dot_nn(spread, grad_low).astype(BF16)
    slot_exchange(packed, arrived, a_send, a_recv, c, n)
    gall[d, m] = dot_nn(collect, arrived[...]).astype(BF16)

    def to_partner(k):
        h = lax.rem(m - k + mp, mp)
        return remote(
            gall.at[d, h], gall.at[d, h], f_send.at[k], f_recv.at[k], {"dp": 1 - d}
        )

    g_copies = {}
    to_partner(0).start()
    for k in order:
        if k:
            g_copies[k] = remote(
                gall.at[d, m],
                gall.at[d, m],
                g_send.at[k],
                g_recv.at[k],
                {"mp": lax.rem(m + k, mp)},
            )
            g_copies[k].start()

    def x_copy(k, kx):
        to = lax.rem(x + kx, nx)
        return remote(
            xs.at[k, to], xr.at[k, kx], x_send.at[k, kx], x_recv.at[k, kx], {"ctx": z * nx + to}
        )

    for k in order:
        h = lax.rem(m - k + mp, mp)
        if k:
            g_copies[k].wait_recv()
            to_partner(k).start()
        to_partner(k).wait_recv()
        for j in range(nx):
            rows = slice(j * chunk, (j + 1) * chunk)
            xs[k, j] = (
                dot_nn(sht[rows, :tokens], gall[0, h]) + dot_nn(sht[rows, tokens:], gall[1, h])
            ).astype(BF16)
        for kx in range(1, nx):
            x_copy(k, kx).start()

    ig = dot_nt(gall[1 - d, 0], wh[0])
    for h in range(1, mp):
        ig = ig + dot_nt(gall[1 - d, h], wh[h])
    ig_send[...] = ig.astype(BF16)
    ig_copy = remote(ig_send, ig_recv, o_sems.at[0], o_sems.at[1], {"dp": 1 - d})
    ig_copy.start()
    ig = dot_nt(gall[d, 0], wh[0])
    for h in range(1, mp):
        ig = ig + dot_nt(gall[d, h], wh[h])
    image_out[:, pl.ds(pl.multiple_of(d * half, half), half)] = ig.astype(BF16)

    def y_copy(k):
        return remote(
            ys.at[k], yr.at[k], y_send.at[k], y_recv.at[k], {"mp": lax.rem(m - k + mp, mp)}
        )

    def z_target(k):
        return 2 * lax.rem(m + k, mp) + d

    def z_copy(k, other):
        e = 1 - d if other else d
        rows = pl.ds(pl.multiple_of(e * part, part), part)
        device = {"ctx": z_target(k) * nx + x}
        if other:
            device["dp"] = 1 - d
        return remote(
            yr.at[k, rows], zr.at[z], z_send.at[k, int(other)], z_recv.at[z], device
        )

    def scatter_z(k):
        z_copy(k, True).start()

        @pl.when(z_target(k) != z)
        def _():
            z_copy(k, False).start()

        @pl.when(z_target(k) == z)
        def _():
            zr[z] = yr[k, pl.ds(pl.multiple_of(d * part, part), part), :]

    for k in order:
        total = xs[k, x].astype(F32)
        for kx in range(1, nx):
            x_copy(k, kx).wait_recv()
            total = total + xr[k, kx].astype(F32)
        if k:
            ys[k] = total.astype(BF16)
            y_copy(k).start()
        else:
            yr[0] = total.astype(BF16)
            scatter_z(0)
    for k in order:
        if k:
            y_copy(k).wait_recv()
            scatter_z(k)

    ig_copy.wait()
    image_out[:, pl.ds(pl.multiple_of((1 - d) * half, half), half)] = ig_recv[...]

    def wait_z(k, carry):
        @pl.when(jnp.logical_or(k != z, lax.rem(z, 2) != d))
        def _():
            remote(
                yr.at[0, pl.ds(0, part)], zr.at[k], z_send.at[0, 0], z_recv.at[k], {"dp": 1 - d}
            ).wait_recv()

        return carry

    lax.fori_loop(0, nz, wait_z, 0)
    total = zr[0].astype(F32)
    for k in range(1, nz):
        total = total + zr[k].astype(F32)
    wg_send[...] = total
    wg_copy = remote(wg_send, wg_recv, o_sems.at[2], o_sems.at[3], {"dp": 1 - d})
    wg_copy.start()
    weight_out[pl.ds(pl.multiple_of(d * part, part), part), :] = total
    wg_copy.wait()
    weight_out[pl.ds(pl.multiple_of((1 - d) * part, part), part), :] = wg_recv[...]

    for k in order:
        to_partner(k).wait_send()
        for kx in range(1, nx):
            x_copy(k, kx).wait_send()
        if k:
            g_copies[k].wait_send()
            y_copy(k).wait_send()
        z_copy(k, True).wait_send()

        @pl.when(z_target(k) != z)
        def _(k=k):
            z_copy(k, False).wait_send()


def gradients(pos_col, slot_col, prev_grad, own_grad, wh, sht, n, mp):
    half, width = wh.shape[1:]
    tokens = slot_col.shape[0]
    size = own_grad.shape[0]
    nx = n // (2 * mp)
    nz = 2 * mp
    chunk = half // nx
    slots = n * IMGTOK
    vmem = pl.BlockSpec(memory_space=pltpu.VMEM)
    dma = pltpu.SemaphoreType.DMA
    return pl.pallas_call(
        functools.partial(grad_kernel, n, mp, nx, nz),
        out_shape=(
            jax.ShapeDtypeStruct((tokens, 2 * half), BF16),
            jax.ShapeDtypeStruct((chunk, width), F32),
        ),
        in_specs=[vmem] * 6,
        out_specs=(vmem, vmem),
        scratch_shapes=[
            pltpu.VMEM((size, width), BF16),
            pltpu.VMEM((slots, width), BF16),
            pltpu.VMEM((slots, width), BF16),
            pltpu.VMEM((2, mp, tokens, width), BF16),
            pltpu.VMEM((mp, nx, chunk, width), BF16),
            pltpu.VMEM((mp, nx, chunk, width), BF16),
            pltpu.VMEM((mp, chunk, width), BF16),
            pltpu.VMEM((mp, chunk, width), BF16),
            pltpu.VMEM((nz, chunk // 2, width), BF16),
            pltpu.VMEM((chunk // 2, width), F32),
            pltpu.VMEM((chunk // 2, width), F32),
            pltpu.VMEM((tokens, half), BF16),
            pltpu.VMEM((tokens, half), BF16),
            dma((2,)),
            dma((n,)),
            dma((n,)),
            dma((mp,)),
            dma((mp,)),
            dma((mp,)),
            dma((mp,)),
            dma((mp, nx)),
            dma((mp, nx)),
            dma((mp,)),
            dma((mp,)),
            dma((mp, 2)),
            dma((nz,)),
            dma((4,)),
        ],
        compiler_params=pltpu.CompilerParams(
            collective_id=1, has_side_effects=True, vmem_limit_bytes=48 << 20
        ),
        name="gradients",
    )(pos_col, slot_col, prev_grad, own_grad, wh, sht)


def per_device(image_states, place_index, doc_ids, queries, text_kv, kv_weight, d_out):
    n = lax.axis_size("ctx")
    mp = lax.axis_size("mp")
    c = lax.axis_index("ctx")
    size = queries.shape[1]
    tokens = image_states.shape[1]
    hd = kv_weight.shape[2] // 2

    place = place_index[0].reshape(n, tokens)
    own_place = lax.dynamic_slice_in_dim(place, c, 1, axis=0)
    slot_row = (own_place // size) * IMGTOK + own_place % IMGTOK
    local = jnp.where(place // size == c, place % size, -1)
    pos = jnp.max(local.reshape(n, tokens // IMGTOK, IMGTOK), axis=1).reshape(1, n * IMGTOK)

    docs = doc_ids[0].reshape(n, size)
    own_docs = lax.dynamic_slice_in_dim(docs, c, 1, axis=0)
    prior_docs = lax.dynamic_slice_in_dim(docs, jnp.maximum(c - 1, 0), 1, axis=0)
    prior_docs = jnp.where(c > 0, prior_docs, -1)
    key_docs = jnp.concatenate([prior_docs, own_docs], axis=1).reshape(2 * size, 1)

    own_kv, prev_kv, wh, sht = route(
        slot_row, pos, text_kv[0], image_states[0], kv_weight[0], n, mp
    )
    attn_out, prev_grad, own_grad = attention(
        own_docs, key_docs, queries[0], d_out[0], prev_kv, own_kv, hd
    )
    image_grad, weight_grad = gradients(
        pos.reshape(-1, 1), slot_row.reshape(-1, 1), prev_grad, own_grad, wh, sht, n, mp
    )
    return (attn_out[None], image_grad[None], weight_grad[None])


def solution(mesh):
    in_specs = (
        P("dp", "ctx", "mp"),
        P("dp", None),
        P("dp", None),
        P("dp", "ctx", "mp"),
        P("dp", "ctx", "mp"),
        P("mp", None, None),
        P("dp", "ctx", "mp"),
    )
    out_specs = (P("dp", "ctx", "mp"), P("dp", "ctx", "mp"), P("mp", "ctx", None))
    return jax.shard_map(
        per_device, mesh=mesh, in_specs=in_specs, out_specs=out_specs, check_vma=False
    )
```

time: 723 us -> 172 us (0.24)
  waiting for transfers between devices: 405 us -> 0 us
  Pallas kernels: 0 us -> 157 us
  local copies, waits for them, and re-layouts: 141 us -> 10.2 us
  matrix products: 84.7 us -> 0 us
  other arithmetic: 49.5 us -> 3.49 us
  starting transfers between devices: 25.9 us -> 0 us
  between operations: 14.1 us -> 0.77 us
    reduce_scatter x2 -> x0, waiting for transfers between devices: 316 us -> none  [the longest x1 236 us: per_device(): lax.psum_scatter(lax.dot_general(state_rows, grad_low, (((0,), (0,)), (()...]
    pallas_call x0 -> x3, Pallas kernels: none -> 157 us  [the longest x1 69.7 us: gradients(): pl.pallas_call(functools.partial(grad_kernel, n, mp, nx, nz), out_shape=(...]
    dot_general x35 -> x0, matrix products: 84.7 us -> none  [the longest x8 21.9 us: one_head(): lax.dot_general(grad_scores, query_head, (((0,), (0,)), ((), ())), prefer...]
    scatter x4 -> x0, local copies, waits for them, and re-layouts: 66.4 us -> none  [the longest x1 30.4 us: routing_tables(): image_marks = jnp.zeros((ctx_dev,), jnp.int32).at[jnp.where(is_mine, loca...]
    gather x4 -> x0, local copies, waits for them, and re-layouts: 57 us -> none  [the longest x1 51.2 us: routing_tables(): compact = jnp.where(is_mine, compact_of_pos[local_pos], image_dev)]
    all_gather x1 -> x0, waiting for transfers between devices: 44.7 us -> none  [per_device(): lax.all_gather(arrived.reshape(rank_count * capacity, arrived.shape[2])[r...]
    psum x1 -> x0, waiting for transfers between devices: 29.8 us -> none  [per_device(): weight_grad = lax.psum(weight_share, 'dp')]
    all_to_all x2 -> x0, starting transfers between devices: 20.6 us -> none  [the longest x1 11 us: per_device(): lax.all_to_all(holder.reshape(rank_count, capacity, own_states.shape[1]),...]
  transfers between devices with their start and end apart: 8 -> 0, of which waited for: 6 -> 0; matrix products, arithmetic and copies ran while one was open for 19% -> 0% of each run, Pallas kernels for 0% -> 0%
where the time goes in v1:
time: 172 us; the launch traced here: 171 us
  Pallas kernels  157 us (91%)
  local copies, waits for them, and re-layouts  10.2 us (6%)
  other arithmetic  3.49 us (2%)
    pallas_call x1, Pallas kernels, gradients(): pl.pallas_call(functools.partial(grad_kernel, n, mp, nx, nz), out_shape=(...  69.7 us
    pallas_call x1, Pallas kernels, route(): pl.pallas_call(functools.partial(route_kernel, n, mp), out_shape=(jax.Sha...  68.5 us
    pallas_call x1, Pallas kernels, attention(): pl.pallas_call(functools.partial(attention_kernel, block), grid=(width //...  18.7 us
    unnamed x17, local copies, waits for them, and re-layouts  8.75 us

profile of v1, /device:TPU:17, one launch (start us, length us, event | category | flops | bytes accessed | tf_op | source)
XLA Modules:
  0.0 171.4 jit_solution(6934916916721269870)
XLA Ops:
  0.6 0.5 broadcast.101
  1.1 1.6 reduce.8
  2.8 0.2 copy.10.k_docs
  3.1 1.5 reduce.9
  4.6 0.9 reshape_squeeze.10
  5.5 0.3 fusion.2
  5.8 0.1 reshape.18.pos_row
  5.9 0.0 copy-start
  5.9 2.2 %copy-done = bf16[1,8192,256]{2,1,0:T(8,128)(2,1)S(1)} copy-done((bf16[1,8192,256]{2,1,0:T(8,128)(2,1)S(1)}, bf16[1,8192,256]{2,1,0:T(8,128)(2,1)}, u32[]{:S(2)}) %copy-start) | copy-done | bytes 4194328
  8.1 0.0 copy-start.1
  8.1 1.2 copy-done.1
  9.3 0.0 copy-start.6
  9.3 0.9 copy-done.6
  10.3 0.0 copy-start.2
  10.3 0.0 copy-start.3
  10.3 68.5 %route.1 = (bf16[512,256]{1,0:T(8,128)(2,1)S(1)}, bf16[512,256]{1,0:T(8,128)(2,1)S(1)}, bf16[4,1024,256]{2,1,0:T(8,128)(2,1)S(1)}, bf16[1024,512]{1,0:T(8,128)(2,1)S(1)}) custom-call(s32[1,256]{1,0:T(1,128)S(1)} %fusion.5.slot_row, s32[1,512]{1,0:T(1,128)S(1)} %reshape.18.pos_row, bf16[512,256]{1,0:T(8,128)(2,1)S(1)} %bitcast.18, ...), custom_call_target="tpu_custom_call" | custom-call | tf_op jit(solution)/shard_map/route/pallas_call | solution.py:238
  78.7 0.0 copy-start.4
  78.8 1.0 copy-done.4
  79.7 0.0 copy-done.2
  79.7 0.0 copy-done.3
  79.7 18.7 %attention.1 = (bf16[512,1024]{1,0:T(8,128)(2,1)}, bf16[512,256]{1,0:T(8,128)(2,1)S(1)}, f32[512,256]{1,0:T(8,128)S(1)}) custom-call(s32[1,512]{1,0:T(1,128)S(1)} %get-tuple-element.22.q_docs, s32[1024,1]{1,0:T(8,128)S(1)} %copy.10.k_docs, bf16[512,1024]{1,0:T(8,128)(2,1)S(1)} %bitcast.16, bf16[512,1024]{1,0:T(8,128)(2,1)S(1)} %bitcast.17, ...), custom_call_target="tpu_custom_call" | custom-call | tf_op jit(solution)/shard_map/attention/pallas_call | solution.py:352
  98.5 0.2 reshape_reshape.4.pos_col
  98.7 0.1 copy.12.slot_col
  98.8 0.0 copy-start.5
  98.8 1.2 copy-done.5
  100.0 69.7 %gradients.1 = (bf16[256,2048]{1,0:T(8,128)(2,1)S(1)}, f32[256,256]{1,0:T(8,128)S(1)}) custom-call(s32[512,1]{1,0:T(8,128)S(1)} %reshape_reshape.4.pos_col, s32[256,1]{1,0:T(8,128)S(1)} %copy.12.slot_col, bf16[512,256]{1,0:T(8,128)(2,1)S(1)} %get-tuple-element.15.prev_grad, f32[512,256]{1,0:T(8,128)S(1)} %get-tuple-element.16.own_grad, ...), custom_call_target="tpu_custom_call" | custom-call | tf_op jit(solution)/shard_map/gradients/pallas_call | solution.py:622
  169.7 1.0 copy.15
  170.7 0.7 copy.16
  (6 shorter events, 0.1 us)
Async XLA Ops:
  5.9 2.2 %copy-start = (bf16[1,8192,256]{2,1,0:T(8,128)(2,1)S(1)}, bf16[1,8192,256]{2,1,0:T(8,128)(2,1)}, u32[]{:S(2)}) copy-start(bf16[1,8192,256]{2,1,0:T(8,128)(2,1)} %param.12) | copy-start | bytes 12582916
  8.1 1.2 copy-start.1
  9.3 0.9 copy-start.6
  10.3 69.5 %copy-start.2 = (bf16[1,512,1024]{2,1,0:T(8,128)(2,1)S(1)}, bf16[1,512,1024]{2,1,0:T(8,128)(2,1)}, u32[]{:S(2)}) copy-start(bf16[1,512,1024]{2,1,0:T(8,128)(2,1)} %param.10) | copy-start | bytes 3145732
  10.3 69.5 %copy-start.3 = (bf16[1,512,1024]{2,1,0:T(8,128)(2,1)S(1)}, bf16[1,512,1024]{2,1,0:T(8,128)(2,1)}, u32[]{:S(2)}) copy-start(bf16[1,512,1024]{2,1,0:T(8,128)(2,1)} %param.13) | copy-start | bytes 3145732
  78.7 1.0 copy-start.4
  98.8 1.2 copy-start.5

commit v2 on v1

v2 whole, which is shorter than its diff:
```python
import functools
import math

import jax
import jax.numpy as jnp
from jax import lax
from jax.experimental import pallas as pl
from jax.experimental.pallas import tpu as pltpu
from jax.sharding import PartitionSpec as P

IMGTOK = 16
BF16 = jnp.bfloat16
F32 = jnp.float32
MESH = pl.DeviceIdType.MESH


def dot_nn(a, b):
    return jnp.dot(a, b, preferred_element_type=F32)


def dot_nt(a, b):
    return lax.dot_general(a, b, (((1,), (1,)), ((), ())), preferred_element_type=F32)


def iota(shape, dim):
    return lax.broadcasted_iota(jnp.int32, shape, dim)


def ring_order(count):
    return sorted(range(count), key=lambda k: (min(k, count - k), k))


def remote(src, dst, send_sem, recv_sem, device):
    return pltpu.make_async_remote_copy(
        src_ref=src,
        dst_ref=dst,
        send_sem=send_sem,
        recv_sem=recv_sem,
        device_id=device,
        device_id_type=MESH,
    )


def slot_exchange(packed, arrived, send_sems, recv_sems, c, n):
    def copy_of(k):
        p = lax.rem(c + k, n)
        return remote(
            packed.at[pl.ds(pl.multiple_of(p * IMGTOK, IMGTOK), IMGTOK)],
            arrived.at[pl.ds(pl.multiple_of(c * IMGTOK, IMGTOK), IMGTOK)],
            send_sems.at[k],
            recv_sems.at[k],
            {"ctx": p},
        )

    def start(k, carry):
        copy_of(k).start()
        return carry

    def finish(k, carry):
        copy_of(k).wait()
        return carry

    lax.fori_loop(1, n, start, 0)
    mine = pl.ds(pl.multiple_of(c * IMGTOK, IMGTOK), IMGTOK)
    arrived[mine, :] = packed[mine, :]
    lax.fori_loop(1, n, finish, 0)


def fused_kernel(
    n,
    mp,
    nx,
    nz,
    hd,
    place_ref,
    docs_ref,
    text_hbm,
    states,
    weights,
    queries,
    grads,
    attn_out,
    image_out,
    weight_out,
    sh,
    wh,
    sht,
    psend,
    precv,
    acc,
    ysend,
    yrecv,
    table,
    pick,
    collect,
    place,
    spread,
    squeeze,
    widen,
    prev_widen,
    prev_squeeze,
    text,
    prev_text,
    packed,
    arrived,
    small,
    small_in,
    q_all,
    g_all,
    out_all,
    bias,
    keys,
    vals,
    vals_t,
    key_sum,
    val_sum,
    small_grad,
    later,
    back,
    gall,
    xs,
    xr,
    ys,
    yr,
    zr,
    wg_send,
    wg_recv,
    ig_send,
    ig_recv,
    local_sems,
    s_sems,
    wa_send,
    wa_recv,
    wb_send,
    wb_recv,
    wc_send,
    wc_recv,
    fx_send,
    fx_recv,
    fz_send,
    fz_recv,
    p_send,
    p_recv,
    i_send,
    i_recv,
    a_send,
    a_recv,
    k_sems,
    b_send,
    b_recv,
    f_send,
    f_recv,
    g_send,
    g_recv,
    x_send,
    x_recv,
    y_send,
    y_recv,
    z_send,
    z_recv,
    o_sems,
):
    c = lax.axis_index("ctx")
    m = lax.axis_index("mp")
    d = lax.axis_index("dp")
    z = c // nx
    x = lax.rem(c, nx)
    order = ring_order(mp)
    tokens, half = sh.shape[1:]
    size = text.shape[0]
    slots = n * IMGTOK
    chunk = half // nx
    part = chunk // 2
    before = lax.rem(c + n - 1, n)

    get_w = pltpu.make_async_copy(
        weights.at[pl.ds(pl.multiple_of(m * 2 * half + d * half, half), half)],
        wh.at[m],
        local_sems.at[0],
    )
    get_s = pltpu.make_async_copy(
        states.at[:, pl.ds(pl.multiple_of(d * half, half), half)], sh.at[d], local_sems.at[1]
    )
    get_text = pltpu.make_async_copy(text_hbm, text, local_sems.at[2])
    get_q = pltpu.make_async_copy(queries, q_all, local_sems.at[3])
    get_g = pltpu.make_async_copy(grads, g_all, local_sems.at[4])
    for copy in (get_w, get_s, get_text, get_q, get_g):
        copy.start()

    barrier = pltpu.get_barrier_semaphore()

    def greet(k, carry):
        pl.semaphore_signal(
            barrier, inc=1, device_id={"ctx": lax.rem(c + k, n)}, device_id_type=MESH
        )
        return carry

    def greet_other(k, carry):
        pl.semaphore_signal(
            barrier,
            inc=1,
            device_id={"dp": 1 - d, "ctx": lax.rem(z + k, nz) * nx + x},
            device_id_type=MESH,
        )
        return carry

    lax.fori_loop(1, n, greet, 0)
    lax.fori_loop(1, nz, greet_other, 0)
    for k in range(1, mp):
        pl.semaphore_signal(
            barrier, inc=1, device_id={"mp": lax.rem(m + k, mp)}, device_id_type=MESH
        )
    pl.semaphore_signal(barrier, inc=1, device_id={"dp": 1 - d}, device_id_type=MESH)
    pl.semaphore_wait(barrier, 1 + (mp - 1) + (n - 1) + (nz - 1))

    rows_a = half // 4
    rows_b = half // 2 // nx
    rows_c = half // 4 // nz
    span_a = pl.ds(0, rows_a)
    first_b = rows_a + x * rows_b
    first_c = rows_a + nx * rows_b + z * rows_c

    def w_copy(k, first, rows, send_sems, recv_sems):
        p = lax.rem(m + k, mp)
        base = p * 2 * half + d * half
        return remote(
            weights.at[pl.ds(pl.multiple_of(base + first, rows), rows)],
            wh.at[m, pl.ds(pl.multiple_of(first, rows), rows)],
            send_sems.at[k],
            recv_sems.at[k],
            {"mp": p},
        )

    far_first = [k for k in reversed(order) if k]
    wc = {k: w_copy(k, first_c, rows_c, wc_send, wc_recv) for k in far_first}
    wb = {k: w_copy(k, first_b, rows_b, wb_send, wb_recv) for k in far_first}
    wa = {k: w_copy(k, 0, rows_a, wa_send, wa_recv) for k in far_first}
    for group in (wc, wb, wa):
        for k in far_first:
            group[k].start()
    s_copy = remote(
        states.at[:, pl.ds(pl.multiple_of((1 - d) * half, half), half)],
        sh.at[d],
        s_sems.at[0],
        s_sems.at[1],
        {"dp": 1 - d},
    )
    s_copy.start()
    get_text.wait()
    text_copy = remote(
        text_hbm, prev_text, k_sems.at[0], k_sems.at[1], {"ctx": lax.rem(c + 1, n)}
    )
    text_copy.start()

    for r in range(n):
        table[r : r + 1, :] = place_ref[:, r * tokens : (r + 1) * tokens]
    own_place = place_ref[:, pl.ds(pl.multiple_of(c * tokens, tokens), tokens)]
    slot_row = lax.div(own_place, size) * IMGTOK + lax.rem(own_place, IMGTOK)
    pick[...] = (iota((slots, tokens), 0) == slot_row).astype(F32).astype(BF16)
    collect[...] = pick[...].T
    fold = (
        (lax.rem(iota((tokens, slots), 0), IMGTOK) == lax.rem(iota((tokens, slots), 1), IMGTOK))
        .astype(F32)
        .astype(BF16)
    )
    earlier = (iota((slots, slots), 0) < iota((slots, slots), 1)).astype(F32).astype(BF16)

    def shard_tables(q):
        marks = jnp.where(
            lax.div(table[...], size) == q, lax.div(lax.rem(table[...], size), IMGTOK) + 1, 0
        )
        sums = dot_nn(marks.astype(F32).astype(BF16), fold)
        of_rank = iota((n, slots), 0) == lax.div(iota((n, slots), 1), IMGTOK)
        row = jnp.sum(jnp.where(of_rank, sums, 0.0), axis=0, keepdims=True)
        valid = row > 0.5
        inside = lax.rem(iota((1, slots), 1), IMGTOK).astype(F32)
        pos = jnp.where(valid, (row - 1.0) * IMGTOK + inside, -1.0)
        to_pos = (iota((size, slots), 0).astype(F32) == pos).astype(F32)
        flags = jnp.broadcast_to(valid.astype(F32), (8, slots)).astype(BF16)
        rank = jnp.where(valid, dot_nn(flags, earlier)[:1], -1.0)
        to_small = (iota((tokens, slots), 0).astype(F32) == rank).astype(F32).astype(BF16)
        return to_pos, to_small

    to_pos, to_small = shard_tables(c)
    is_image = jnp.sum(to_pos, axis=1, keepdims=True) > 0.5
    text[...] = jnp.where(is_image, 0.0, text[...].astype(F32)).astype(BF16)
    place[...] = to_pos.astype(BF16)
    spread[...] = place[...].T
    squeeze[...] = to_small
    widen[...] = dot_nt(place[...], to_small).astype(BF16)
    to_pos, to_small = shard_tables(before)
    is_prev_image = jnp.sum(to_pos, axis=1, keepdims=True) > 0.5
    prev_widen[...] = dot_nt(to_pos.astype(BF16), to_small).astype(BF16)
    prev_squeeze[...] = prev_widen[...].T

    own_docs = docs_ref[:, pl.ds(pl.multiple_of(c * size, size), size)].astype(F32)
    prior_docs = docs_ref[:, pl.ds(pl.multiple_of(before * size, size), size)].astype(F32)
    prior_docs = jnp.where(c > 0, prior_docs, -1.0)
    diagonal = iota((size, size), 0) == iota((size, size), 1)
    block = size // 2
    span = size + block
    own_col = jnp.sum(jnp.where(diagonal, own_docs, 0.0), axis=1, keepdims=True)
    prior_col = jnp.sum(jnp.where(diagonal, prior_docs, 0.0), axis=1, keepdims=True)
    for i in range(2):
        first = i * block
        docs_col = jnp.concatenate([prior_col[first:], own_col[: first + block]], axis=0)
        key_pos = iota((span, block), 0) + (first - size)
        query_pos = iota((span, block), 1) + first
        allowed = (key_pos <= query_pos) & (docs_col == own_docs[:, first : first + block])
        bias[i] = jnp.where(allowed, 0.0, -1e30)
    key_sum[...] = jnp.zeros_like(key_sum)
    val_sum[...] = jnp.zeros_like(val_sum)

    def fx_copy(k, kx):
        rows = pl.ds(pl.multiple_of(first_b, rows_b), rows_b)
        h = lax.rem(m - k + mp, mp)
        return remote(
            wh.at[h, rows],
            wh.at[h, rows],
            fx_send.at[k, kx],
            fx_recv.at[k, kx],
            {"ctx": z * nx + lax.rem(x + kx, nx)},
        )

    def fz_copy(k, kz):
        rows = pl.ds(pl.multiple_of(first_c, rows_c), rows_c)
        h = lax.rem(m - k + mp, mp)
        return remote(
            wh.at[h, rows],
            wh.at[h, rows],
            fz_send.at[k, kz],
            fz_recv.at[k, kz],
            {"ctx": lax.rem(z + kz, nz) * nx + x},
        )

    def each_z(k, action):
        def body(kz, carry):
            action(fz_copy(k, kz))
            return carry

        lax.fori_loop(1, nz, body, 0)

    near_first = [k for k in order if k]
    for k in near_first:
        wc[k].wait_recv()
        each_z(k, lambda copy: copy.start())
        wb[k].wait_recv()
        for kx in range(1, nx):
            fx_copy(k, kx).start()

    get_s.wait()
    get_w.wait()
    s_copy.wait()
    for b in range(2):
        sht[:, b * tokens : (b + 1) * tokens] = sh[b].T
    text_copy.wait()
    prev_text[...] = jnp.where(is_prev_image, 0.0, prev_text[...].astype(F32)).astype(BF16)

    p_copies = {}
    for k in order:
        h = lax.rem(m - k + mp, mp)
        if k:
            wa[k].wait_recv()
            for kx in range(1, nx):
                fx_copy(k, kx).wait_recv()
            each_z(k, lambda copy: copy.wait_recv())
        psend[k] = dot_nn(sh[1 - d], wh[h])
        p_copies[k] = remote(
            psend.at[k], precv.at[k], p_send.at[k], p_recv.at[k], {"dp": 1 - d}
        )
        p_copies[k].start()
        acc[k] = dot_nn(sh[d], wh[h])

    i_copies = {}
    for k in order:
        p_copies[k].wait_recv()
        if k:
            ysend[k] = (acc[k] + precv[k]).astype(BF16)
            i_copies[k] = remote(
                ysend.at[k],
                yrecv.at[k],
                i_send.at[k],
                i_recv.at[k],
                {"mp": lax.rem(m - k + mp, mp)},
            )
            i_copies[k].start()
    total = acc[0] + precv[0]
    for k in near_first:
        i_copies[k].wait_recv()
        total = total + yrecv[k].astype(F32)

    packed[...] = dot_nn(pick[...], total.astype(BF16)).astype(BF16)
    slot_exchange(packed, arrived, a_send, a_recv, c, n)
    small[...] = dot_nn(squeeze[...], arrived[...]).astype(BF16)
    shift = remote(small, small_in, k_sems.at[2], k_sems.at[3], {"ctx": lax.rem(c + 1, n)})
    shift.start()
    own_kv = (dot_nn(place[...], arrived[...]) + text[...].astype(F32)).astype(BF16)
    keys[size:] = own_kv[:, :hd]
    vals[size:] = own_kv[:, hd:]
    get_q.wait()
    get_g.wait()
    shift.wait()
    prev_kv = (dot_nn(prev_widen[...], small_in[...]) + prev_text[...].astype(F32)).astype(BF16)
    keys[:size] = prev_kv[:, :hd]
    vals[:size] = prev_kv[:, hd:]
    vals_t[...] = vals[...].T

    scale = hd ** (-0.5)
    to_log2 = scale / math.log(2.0)

    def one_head(head, carry):
        lanes = pl.ds(pl.multiple_of(head * hd, hd), hd)
        for i in range(2):
            first = i * block
            rows = slice(first, first + block)
            window = slice(first, first + span)
            q = q_all[rows, lanes]
            g = g_all[rows, lanes]
            scores = dot_nt(keys[window, :], q) * to_log2 + bias[i]
            shifted = jnp.exp2(scores - jnp.max(scores, axis=0, keepdims=True))
            probs = shifted * (1.0 / jnp.sum(shifted, axis=0, keepdims=True))
            low = probs.astype(BF16)
            context = dot_nn(vals_t[:, window], low)
            grad_probs = dot_nt(vals[window, :], g)
            delta = jnp.sum(g.T.astype(F32) * context, axis=0, keepdims=True)
            grad_scores = (probs * (grad_probs - delta)).astype(BF16)
            out_all[rows, lanes] = context.T.astype(BF16)
            key_sum[window, :] += dot_nn(grad_scores, q)
            val_sum[window, :] += dot_nn(low, g)
        return carry

    lax.fori_loop(0, q_all.shape[1] // hd, one_head, 0)
    put_out = pltpu.make_async_copy(out_all, attn_out, local_sems.at[5])

    prev_grad = jnp.concatenate(
        [(key_sum[:size] * scale).astype(BF16), val_sum[:size].astype(BF16)], axis=1
    )
    small_grad[...] = dot_nn(prev_squeeze[...], prev_grad).astype(BF16)
    back_shift = remote(small_grad, later, k_sems.at[4], k_sems.at[5], {"ctx": before})
    back_shift.start()
    put_out.start()
    own_grad = jnp.concatenate([key_sum[size:] * scale, val_sum[size:]], axis=1)
    back_shift.wait()
    grad_low = (own_grad + dot_nn(widen[...], later[...])).astype(BF16)
    packed[...] = dot_nn(spread[...], grad_low).astype(BF16)
    slot_exchange(packed, back, b_send, b_recv, c, n)
    gall[d, m] = dot_nn(collect[...], back[...]).astype(BF16)

    def to_partner(k):
        h = lax.rem(m - k + mp, mp)
        return remote(
            gall.at[d, h], gall.at[d, h], f_send.at[k], f_recv.at[k], {"dp": 1 - d}
        )

    g_copies = {}
    to_partner(0).start()
    for k in order:
        if k:
            g_copies[k] = remote(
                gall.at[d, m],
                gall.at[d, m],
                g_send.at[k],
                g_recv.at[k],
                {"mp": lax.rem(m + k, mp)},
            )
            g_copies[k].start()

    def x_copy(k, kx):
        to = lax.rem(x + kx, nx)
        return remote(
            xs.at[k, to], xr.at[k, kx], x_send.at[k, kx], x_recv.at[k, kx], {"ctx": z * nx + to}
        )

    for k in order:
        h = lax.rem(m - k + mp, mp)
        if k:
            g_copies[k].wait_recv()
            to_partner(k).start()
        to_partner(k).wait_recv()
        for j in range(nx):
            rows = slice(j * chunk, (j + 1) * chunk)
            xs[k, j] = (
                dot_nn(sht[rows, :tokens], gall[0, h]) + dot_nn(sht[rows, tokens:], gall[1, h])
            ).astype(BF16)
        for kx in range(1, nx):
            x_copy(k, kx).start()

    ig = dot_nt(gall[1 - d, 0], wh[0])
    for h in range(1, mp):
        ig = ig + dot_nt(gall[1 - d, h], wh[h])
    ig_send[...] = ig.astype(BF16)
    ig_copy = remote(ig_send, ig_recv, o_sems.at[0], o_sems.at[1], {"dp": 1 - d})
    ig_copy.start()
    ig = dot_nt(gall[d, 0], wh[0])
    for h in range(1, mp):
        ig = ig + dot_nt(gall[d, h], wh[h])
    image_out[:, pl.ds(pl.multiple_of(d * half, half), half)] = ig.astype(BF16)

    def y_copy(k):
        return remote(
            ys.at[k], yr.at[k], y_send.at[k], y_recv.at[k], {"mp": lax.rem(m - k + mp, mp)}
        )

    def z_target(k):
        return 2 * lax.rem(m + k, mp) + d

    def z_copy(k, other):
        e = 1 - d if other else d
        rows = pl.ds(pl.multiple_of(e * part, part), part)
        device = {"ctx": z_target(k) * nx + x}
        if other:
            device["dp"] = 1 - d
        return remote(
            yr.at[k, rows], zr.at[z], z_send.at[k, int(other)], z_recv.at[z], device
        )

    def scatter_z(k):
        z_copy(k, True).start()

        @pl.when(z_target(k) != z)
        def _():
            z_copy(k, False).start()

        @pl.when(z_target(k) == z)
        def _():
            zr[z] = yr[k, pl.ds(pl.multiple_of(d * part, part), part), :]

    for k in order:
        total = xs[k, x].astype(F32)
        for kx in range(1, nx):
            x_copy(k, kx).wait_recv()
            total = total + xr[k, kx].astype(F32)
        if k:
            ys[k] = total.astype(BF16)
            y_copy(k).start()
        else:
            yr[0] = total.astype(BF16)
            scatter_z(0)
    for k in order:
        if k:
            y_copy(k).wait_recv()
            scatter_z(k)

    ig_copy.wait()
    image_out[:, pl.ds(pl.multiple_of((1 - d) * half, half), half)] = ig_recv[...]

    def wait_z(k, carry):
        @pl.when(jnp.logical_or(k != z, lax.rem(z, 2) != d))
        def _():
            remote(
                yr.at[0, pl.ds(0, part)], zr.at[k], z_send.at[0, 0], z_recv.at[k], {"dp": 1 - d}
            ).wait_recv()

        return carry

    lax.fori_loop(0, nz, wait_z, 0)
    total = zr[0].astype(F32)
    for k in range(1, nz):
        total = total + zr[k].astype(F32)
    wg_send[...] = total
    wg_copy = remote(wg_send, wg_recv, o_sems.at[2], o_sems.at[3], {"dp": 1 - d})
    wg_copy.start()
    weight_out[pl.ds(pl.multiple_of(d * part, part), part), :] = total
    wg_copy.wait()
    weight_out[pl.ds(pl.multiple_of((1 - d) * part, part), part), :] = wg_recv[...]

    for k in order:
        p_copies[k].wait_send()
        to_partner(k).wait_send()
        for kx in range(1, nx):
            x_copy(k, kx).wait_send()
        if k:
            for group in (wa, wb, wc, i_copies, g_copies):
                group[k].wait_send()
            y_copy(k).wait_send()
            for kx in range(1, nx):
                fx_copy(k, kx).wait_send()
            each_z(k, lambda copy: copy.wait_send())
        z_copy(k, True).wait_send()

        @pl.when(z_target(k) != z)
        def _(k=k):
            z_copy(k, False).wait_send()
    put_out.wait()


def fused(place, docs, text, states, weights, queries, grads, n, mp):
    tokens, slice_width = states.shape
    half = slice_width // 2
    width = weights.shape[1]
    hd = width // 2
    size, heads_width = queries.shape
    block = size // 2
    slots = n * IMGTOK
    nx = n // (2 * mp)
    nz = 2 * mp
    chunk = half // nx
    vmem = pl.BlockSpec(memory_space=pltpu.VMEM)
    hbm = pl.BlockSpec(memory_space=pl.ANY)
    dma = pltpu.SemaphoreType.DMA
    low = lambda *shape: pltpu.VMEM(shape, BF16)
    wide = lambda *shape: pltpu.VMEM(shape, F32)
    return pl.pallas_call(
        functools.partial(fused_kernel, n, mp, nx, nz, hd),
        out_shape=(
            jax.ShapeDtypeStruct((size, heads_width), BF16),
            jax.ShapeDtypeStruct((tokens, slice_width), BF16),
            jax.ShapeDtypeStruct((chunk, width), F32),
        ),
        in_specs=[vmem, vmem, hbm, hbm, hbm, hbm, hbm],
        out_specs=(hbm, vmem, vmem),
        scratch_shapes=[
            low(2, tokens, half),
            low(mp, half, width),
            low(half, 2 * tokens),
            wide(mp, tokens, width),
            wide(mp, tokens, width),
            wide(mp, tokens, width),
            low(mp, tokens, width),
            low(mp, tokens, width),
            pltpu.VMEM((n, tokens), jnp.int32),
            low(slots, tokens),
            low(tokens, slots),
            low(size, slots),
            low(slots, size),
            low(tokens, slots),
            low(size, tokens),
            low(size, tokens),
            low(tokens, size),
            low(size, width),
            low(size, width),
            low(slots, width),
            low(slots, width),
            low(tokens, width),
            low(tokens, width),
            low(size, heads_width),
            low(size, heads_width),
            low(size, heads_width),
            wide(2, size + block, block),
            low(2 * size, hd),
            low(2 * size, hd),
            low(hd, 2 * size),
            wide(2 * size, hd),
            wide(2 * size, hd),
            low(tokens, width),
            low(tokens, width),
            low(slots, width),
            low(2, mp, tokens, width),
            low(mp, nx, chunk, width),
            low(mp, nx, chunk, width),
            low(mp, chunk, width),
            low(mp, chunk, width),
            low(nz, chunk // 2, width),
            wide(chunk // 2, width),
            wide(chunk // 2, width),
            low(tokens, half),
            low(tokens, half),
            dma((6,)),
            dma((2,)),
            *[dma((mp,))] * 6,
            *[dma((mp, nx))] * 2,
            *[dma((mp, nz))] * 2,
            *[dma((mp,))] * 4,
            *[dma((n,))] * 2,
            dma((6,)),
            *[dma((n,))] * 2,
            *[dma((mp,))] * 4,
            *[dma((mp, nx))] * 2,
            *[dma((mp,))] * 2,
            dma((mp, 2)),
            dma((nz,)),
            dma((4,)),
        ],
        compiler_params=pltpu.CompilerParams(
            collective_id=0, has_side_effects=True, vmem_limit_bytes=62 << 20
        ),
        name="fused",
    )(place, docs, text, states, weights, queries, grads)


def per_device(image_states, place_index, doc_ids, queries, text_kv, kv_weight, d_out):
    attn_out, image_grad, weight_grad = fused(
        place_index,
        doc_ids,
        text_kv[0],
        image_states[0],
        kv_weight[0],
        queries[0],
        d_out[0],
        lax.axis_size("ctx"),
        lax.axis_size("mp"),
    )
    return (attn_out[None], image_grad[None], weight_grad[None])


def solution(mesh):
    in_specs = (
        P("dp", "ctx", "mp"),
        P("dp", None),
        P("dp", None),
        P("dp", "ctx", "mp"),
        P("dp", "ctx", "mp"),
        P("mp", None, None),
        P("dp", "ctx", "mp"),
    )
    out_specs = (P("dp", "ctx", "mp"), P("dp", "ctx", "mp"), P("mp", "ctx", None))
    return jax.shard_map(
        per_device, mesh=mesh, in_specs=in_specs, out_specs=out_specs, check_vma=False
    )
```

time: 172 us -> 138 us (0.80)
  Pallas kernels: 157 us -> 132 us
  local copies, waits for them, and re-layouts: 10.2 us -> 5.31 us
  other arithmetic: 3.49 us -> 0 us
    pallas_call x3 -> x1, Pallas kernels: 157 us -> 132 us  [fused(): pl.pallas_call(functools.partial(fused_kernel, n, mp, nx, nz, hd), out_sh...]
    unnamed x17 -> x5, local copies, waits for them, and re-layouts: 8.75 us -> 5.31 us
    unnamed x2 -> x0, other arithmetic: 3.13 us -> none
where the time goes in v2:
time: 138 us
  Pallas kernels  132 us (96%)
  local copies, waits for them, and re-layouts  5.31 us (4%)
    pallas_call x1, Pallas kernels, fused(): pl.pallas_call(functools.partial(fused_kernel, n, mp, nx, nz, hd), out_sh...  132 us
    unnamed x5, local copies, waits for them, and re-layouts  5.31 us

profile of v2, /device:TPU:17, one launch (start us, length us, event | category | flops | bytes accessed | tf_op | source)
XLA Modules:
  0.0 138.1 jit_solution(16511484960840407628)
XLA Ops:
  0.6 132.1 %fused.1 = (bf16[512,1024]{1,0:T(8,128)(2,1)}, bf16[256,2048]{1,0:T(8,128)(2,1)}, f32[256,256]{1,0:T(8,128)}) custom-call(s32[1,8192]{1,0:T(1,128)} %place_ref.1, s32[1,16384]{1,0:T(1,128)} %docs_ref.1, bf16[512,256]{1,0:T(8,128)(2,1)} %bitcast.15, bf16[256,2048]{1,0:T(8,128)(2,1)} %bitcast.11, bf16[8192,256]{1,0:T(8,128)(2,1)} %bitcast.8, ...), custom_call_target="tpu_custom_call" | custom-call | tf_op jit(solution)/shard_map/fused/pallas_call | solution.py:603
  132.8 0.0 copy-start
  132.8 2.3 %copy.13 = bf16[1,512,1024]{2,1,0:T(8,128)(2,1)} copy(bf16[1,512,1024]{2,1,0:T(8,128)(2,1)} %bitcast.10) | data formatting | bytes 2097152
  135.1 2.3 %copy.14 = bf16[1,256,2048]{2,1,0:T(8,128)(2,1)} copy(bf16[1,256,2048]{2,1,0:T(8,128)(2,1)} %bitcast.9) | data formatting | bytes 2097152
  137.4 0.0 copy-done
  137.4 0.7 copy.15
Async XLA Ops:
  132.8 4.6 %copy-start = (f32[256,256]{1,0:T(8,128)S(1)}, f32[256,256]{1,0:T(8,128)}, u32[]{:S(2)}) copy-start(f32[256,256]{1,0:T(8,128)} %get-tuple-element.8) | copy-start | bytes 786436

commit v3 on v2

--- a/solution.py
+++ b/solution.py
@@ -112,15 +112,17 @@
     keys,
     vals,
     vals_t,
-    key_sum,
-    val_sum,
+    q_stack,
+    g_stack,
+    low_all,
+    ds_all,
     small_grad,
     later,
     back,
     gall,
     xs,
-    xr,
-    ys,
+    xa,
+    xb,
     yr,
     zr,
     wg_send,
@@ -154,8 +156,8 @@
     g_recv,
     x_send,
     x_recv,
-    y_send,
-    y_recv,
+    t_send,
+    t_recv,
     z_send,
     z_recv,
     o_sems,
@@ -173,6 +175,8 @@
     part = chunk // 2
     before = lax.rem(c + n - 1, n)
 
+    pending = []
+
     get_w = pltpu.make_async_copy(
         weights.at[pl.ds(pl.multiple_of(m * 2 * half + d * half, half), half)],
         wh.at[m],
@@ -211,46 +215,6 @@
             barrier, inc=1, device_id={"mp": lax.rem(m + k, mp)}, device_id_type=MESH
         )
     pl.semaphore_signal(barrier, inc=1, device_id={"dp": 1 - d}, device_id_type=MESH)
-    pl.semaphore_wait(barrier, 1 + (mp - 1) + (n - 1) + (nz - 1))
-
-    rows_a = half // 4
-    rows_b = half // 2 // nx
-    rows_c = half // 4 // nz
-    span_a = pl.ds(0, rows_a)
-    first_b = rows_a + x * rows_b
-    first_c = rows_a + nx * rows_b + z * rows_c
-
-    def w_copy(k, first, rows, send_sems, recv_sems):
-        p = lax.rem(m + k, mp)
-        base = p * 2 * half + d * half
-        return remote(
-            weights.at[pl.ds(pl.multiple_of(base + first, rows), rows)],
-            wh.at[m, pl.ds(pl.multiple_of(first, rows), rows)],
-            send_sems.at[k],
-            recv_sems.at[k],
-            {"mp": p},
-        )
-
-    far_first = [k for k in reversed(order) if k]
-    wc = {k: w_copy(k, first_c, rows_c, wc_send, wc_recv) for k in far_first}
-    wb = {k: w_copy(k, first_b, rows_b, wb_send, wb_recv) for k in far_first}
-    wa = {k: w_copy(k, 0, rows_a, wa_send, wa_recv) for k in far_first}
-    for group in (wc, wb, wa):
-        for k in far_first:
-            group[k].start()
-    s_copy = remote(
-        states.at[:, pl.ds(pl.multiple_of((1 - d) * half, half), half)],
-        sh.at[d],
-        s_sems.at[0],
-        s_sems.at[1],
-        {"dp": 1 - d},
-    )
-    s_copy.start()
-    get_text.wait()
-    text_copy = remote(
-        text_hbm, prev_text, k_sems.at[0], k_sems.at[1], {"ctx": lax.rem(c + 1, n)}
-    )
-    text_copy.start()
 
     for r in range(n):
         table[r : r + 1, :] = place_ref[:, r * tokens : (r + 1) * tokens]
@@ -282,16 +246,99 @@
         return to_pos, to_small
 
     to_pos, to_small = shard_tables(c)
+    get_text.wait()
     is_image = jnp.sum(to_pos, axis=1, keepdims=True) > 0.5
     text[...] = jnp.where(is_image, 0.0, text[...].astype(F32)).astype(BF16)
     place[...] = to_pos.astype(BF16)
     spread[...] = place[...].T
     squeeze[...] = to_small
     widen[...] = dot_nt(place[...], to_small).astype(BF16)
+
+    pl.semaphore_wait(barrier, 1 + (mp - 1) + (n - 1) + (nz - 1))
+
+    rows_a = half // 4
+    rows_b = half // 2 // nx
+    rows_c = half // 4 // nz
+    span_a = pl.ds(0, rows_a)
+    first_b = rows_a + x * rows_b
+    first_c = rows_a + nx * rows_b + z * rows_c
+
+    def w_copy(k, first, rows, send_sems, recv_sems):
+        p = lax.rem(m + k, mp)
+        base = p * 2 * half + d * half
+        return remote(
+            weights.at[pl.ds(pl.multiple_of(base + first, rows), rows)],
+            wh.at[m, pl.ds(pl.multiple_of(first, rows), rows)],
+            send_sems.at[k],
+            recv_sems.at[k],
+            {"mp": p},
+        )
+
+    far_first = [k for k in reversed(order) if k]
+    wc = {k: w_copy(k, first_c, rows_c, wc_send, wc_recv) for k in far_first}
+    wb = {k: w_copy(k, first_b, rows_b, wb_send, wb_recv) for k in far_first}
+    wa = {k: w_copy(k, 0, rows_a, wa_send, wa_recv) for k in far_first}
+    for group in (wc, wb, wa):
+        for k in far_first:
+            group[k].start()
+            pending.append(group[k].wait_send)
+    s_copy = remote(
+        states.at[:, pl.ds(pl.multiple_of((1 - d) * half, half), half)],
+        sh.at[d],
+        s_sems.at[0],
+        s_sems.at[1],
+        {"dp": 1 - d},
+    )
+    s_copy.start()
+    text_copy = remote(
+        text_hbm, prev_text, k_sems.at[0], k_sems.at[1], {"ctx": lax.rem(c + 1, n)}
+    )
+    text_copy.start()
+
     to_pos, to_small = shard_tables(before)
     is_prev_image = jnp.sum(to_pos, axis=1, keepdims=True) > 0.5
     prev_widen[...] = dot_nt(to_pos.astype(BF16), to_small).astype(BF16)
     prev_squeeze[...] = prev_widen[...].T
+
+    def fx_copy(k, kx):
+        rows = pl.ds(pl.multiple_of(first_b, rows_b), rows_b)
+        h = lax.rem(m - k + mp, mp)
+        return remote(
+            wh.at[h, rows],
+            wh.at[h, rows],
+            fx_send.at[k, kx],
+            fx_recv.at[k, kx],
+            {"ctx": z * nx + lax.rem(x + kx, nx)},
+        )
+
+    def fz_copy(k, kz):
+        rows = pl.ds(pl.multiple_of(first_c, rows_c), rows_c)
+        h = lax.rem(m - k + mp, mp)
+        return remote(
+            wh.at[h, rows],
+            wh.at[h, rows],
+            fz_send.at[k, kz],
+            fz_recv.at[k, kz],
+            {"ctx": lax.rem(z + kz, nz) * nx + x},
+        )
+
+    def each_z(k, action):
+        def body(kz, carry):
+            action(fz_copy(k, kz))
+            return carry
+
+        lax.fori_loop(1, nz, body, 0)
+
+    near_first = [k for k in order if k]
+    for k in near_first:
+        wc[k].wait_recv()
+        each_z(k, lambda copy: copy.start())
+        pending.append(functools.partial(each_z, k, lambda copy: copy.wait_send()))
+        wb[k].wait_recv()
+        for kx in range(1, nx):
+            fx_copy(k, kx).start()
+            pending.append(fx_copy(k, kx).wait_send)
+
 
     own_docs = docs_ref[:, pl.ds(pl.multiple_of(c * size, size), size)].astype(F32)
     prior_docs = docs_ref[:, pl.ds(pl.multiple_of(before * size, size), size)].astype(F32)
@@ -308,51 +355,22 @@
         query_pos = iota((span, block), 1) + first
         allowed = (key_pos <= query_pos) & (docs_col == own_docs[:, first : first + block])
         bias[i] = jnp.where(allowed, 0.0, -1e30)
-    key_sum[...] = jnp.zeros_like(key_sum)
-    val_sum[...] = jnp.zeros_like(val_sum)
-
-    def fx_copy(k, kx):
-        rows = pl.ds(pl.multiple_of(first_b, rows_b), rows_b)
-        h = lax.rem(m - k + mp, mp)
-        return remote(
-            wh.at[h, rows],
-            wh.at[h, rows],
-            fx_send.at[k, kx],
-            fx_recv.at[k, kx],
-            {"ctx": z * nx + lax.rem(x + kx, nx)},
-        )
-
-    def fz_copy(k, kz):
-        rows = pl.ds(pl.multiple_of(first_c, rows_c), rows_c)
-        h = lax.rem(m - k + mp, mp)
-        return remote(
-            wh.at[h, rows],
-            wh.at[h, rows],
-            fz_send.at[k, kz],
-            fz_recv.at[k, kz],
-            {"ctx": lax.rem(z + kz, nz) * nx + x},
-        )
-
-    def each_z(k, action):
-        def body(kz, carry):
-            action(fz_copy(k, kz))
-            return carry
-
-        lax.fori_loop(1, nz, body, 0)
-
-    near_first = [k for k in order if k]
-    for k in near_first:
-        wc[k].wait_recv()
-        each_z(k, lambda copy: copy.start())
-        wb[k].wait_recv()
-        for kx in range(1, nx):
-            fx_copy(k, kx).start()
+
+    get_q.wait()
+    get_g.wait()
+    heads = q_all.shape[1] // hd
+    for i in range(2):
+        for head in range(heads):
+            rows = slice(i * block, (i + 1) * block)
+            lanes = slice(head * hd, (head + 1) * hd)
+            q_stack[i, head * block : (head + 1) * block, :] = q_all[rows, lanes]
+            g_stack[i, head * block : (head + 1) * block, :] = g_all[rows, lanes]
 
     get_s.wait()
     get_w.wait()
     s_copy.wait()
     for b in range(2):
-        sht[:, b * tokens : (b + 1) * tokens] = sh[b].T
+        sht[m, :, b * tokens : (b + 1) * tokens] = sh[b].T
     text_copy.wait()
     prev_text[...] = jnp.where(is_prev_image, 0.0, prev_text[...].astype(F32)).astype(BF16)
 
@@ -369,6 +387,7 @@
             psend.at[k], precv.at[k], p_send.at[k], p_recv.at[k], {"dp": 1 - d}
         )
         p_copies[k].start()
+        pending.append(p_copies[k].wait_send)
         acc[k] = dot_nn(sh[d], wh[h])
 
     i_copies = {}
@@ -384,10 +403,19 @@
                 {"mp": lax.rem(m - k + mp, mp)},
             )
             i_copies[k].start()
+            pending.append(i_copies[k].wait_send)
     total = acc[0] + precv[0]
     for k in near_first:
         i_copies[k].wait_recv()
         total = total + yrecv[k].astype(F32)
+
+    s_gather = {}
+    for k in far_first:
+        s_gather[k] = remote(
+            sht.at[m], sht.at[m], t_send.at[k], t_recv.at[k], {"mp": lax.rem(m + k, mp)}
+        )
+        s_gather[k].start()
+        pending.append(s_gather[k].wait_send)
 
     packed[...] = dot_nn(pick[...], total.astype(BF16)).astype(BF16)
     slot_exchange(packed, arrived, a_send, a_recv, c, n)
@@ -397,8 +425,6 @@
     own_kv = (dot_nn(place[...], arrived[...]) + text[...].astype(F32)).astype(BF16)
     keys[size:] = own_kv[:, :hd]
     vals[size:] = own_kv[:, hd:]
-    get_q.wait()
-    get_g.wait()
     shift.wait()
     prev_kv = (dot_nn(prev_widen[...], small_in[...]) + prev_text[...].astype(F32)).astype(BF16)
     keys[:size] = prev_kv[:, :hd]
@@ -410,36 +436,48 @@
 
     def one_head(head, carry):
         lanes = pl.ds(pl.multiple_of(head * hd, hd), hd)
+        stack = pl.ds(pl.multiple_of(head * block, block), block)
         for i in range(2):
             first = i * block
-            rows = slice(first, first + block)
             window = slice(first, first + span)
-            q = q_all[rows, lanes]
-            g = g_all[rows, lanes]
+            q = q_stack[i, stack, :]
+            g = g_stack[i, stack, :]
             scores = dot_nt(keys[window, :], q) * to_log2 + bias[i]
             shifted = jnp.exp2(scores - jnp.max(scores, axis=0, keepdims=True))
             probs = shifted * (1.0 / jnp.sum(shifted, axis=0, keepdims=True))
             low = probs.astype(BF16)
+            low_all[i, :, stack] = low
             context = dot_nn(vals_t[:, window], low)
             grad_probs = dot_nt(vals[window, :], g)
             delta = jnp.sum(g.T.astype(F32) * context, axis=0, keepdims=True)
-            grad_scores = (probs * (grad_probs - delta)).astype(BF16)
-            out_all[rows, lanes] = context.T.astype(BF16)
-            key_sum[window, :] += dot_nn(grad_scores, q)
-            val_sum[window, :] += dot_nn(low, g)
+            ds_all[i, :, stack] = (probs * (grad_probs - delta)).astype(BF16)
+            out_all[first : first + block, lanes] = context.T.astype(BF16)
         return carry
 
-    lax.fori_loop(0, q_all.shape[1] // hd, one_head, 0)
+    lax.fori_loop(0, heads, one_head, 0)
     put_out = pltpu.make_async_copy(out_all, attn_out, local_sems.at[5])
 
+    def prev_sum(left, right):
+        both = dot_nn(left[0, :size, :], right[0])
+        second = dot_nn(left[1, :block, :], right[1])
+        return jnp.concatenate([both[:block], both[block:] + second], axis=0)
+
+    def own_sum(left, right):
+        both = dot_nn(left[1, block:, :], right[1])
+        second = dot_nn(left[0, size:, :], right[0])
+        return jnp.concatenate([both[:block] + second, both[block:]], axis=0)
+
     prev_grad = jnp.concatenate(
-        [(key_sum[:size] * scale).astype(BF16), val_sum[:size].astype(BF16)], axis=1
-    )
+        [prev_sum(ds_all, q_stack) * scale, prev_sum(low_all, g_stack)], axis=1
+    ).astype(BF16)
     small_grad[...] = dot_nn(prev_squeeze[...], prev_grad).astype(BF16)
     back_shift = remote(small_grad, later, k_sems.at[4], k_sems.at[5], {"ctx": before})
     back_shift.start()
     put_out.start()
-    own_grad = jnp.concatenate([key_sum[size:] * scale, val_sum[size:]], axis=1)
+    pending.append(put_out.wait)
+    own_grad = jnp.concatenate(
+        [own_sum(ds_all, q_stack) * scale, own_sum(low_all, g_stack)], axis=1
+    )
     back_shift.wait()
     grad_low = (own_grad + dot_nn(widen[...], later[...])).astype(BF16)
     packed[...] = dot_nn(spread[...], grad_low).astype(BF16)
@@ -454,6 +492,7 @@
 
     g_copies = {}
     to_partner(0).start()
+    pending.append(to_partner(0).wait_send)
     for k in order:
         if k:
             g_copies[k] = remote(
@@ -464,27 +503,109 @@
                 {"mp": lax.rem(m + k, mp)},
             )
             g_copies[k].start()
-
-    def x_copy(k, kx):
-        to = lax.rem(x + kx, nx)
+            pending.append(g_copies[k].wait_send)
+
+    to_partner(0).wait_recv()
+    right, left, opposite = (lax.rem(x + kx, nx) for kx in (1, nx - 1, 2))
+    top, bottom = pl.ds(0, part), pl.ds(part, part)
+
+    def x_copy(k, kind):
+        to_right = kind % 2 == 0
+        near = right if to_right else left
+        side = 0 if to_right else 1
+        if kind < 2:
+            src = xs.at[k, opposite, top if to_right else bottom]
+            dst = xa.at[k, side]
+        else:
+            rows = top if (kind < 4) != to_right else bottom
+            src = xs.at[k, near, rows]
+            dst = xb.at[k, side, rows]
         return remote(
-            xs.at[k, to], xr.at[k, kx], x_send.at[k, kx], x_recv.at[k, kx], {"ctx": z * nx + to}
-        )
-
-    for k in order:
-        h = lax.rem(m - k + mp, mp)
+            src, dst, x_send.at[k, kind], x_recv.at[k, kind], {"ctx": z * nx + near}
+        )
+
+    def start_x(k, kinds):
+        for kind in kinds:
+            x_copy(k, kind).start()
+            pending.append(x_copy(k, kind).wait_send)
+
+    def partial_terms(k):
         if k:
-            g_copies[k].wait_recv()
-            to_partner(k).start()
+            s_gather[k].wait_recv()
+        s = lax.rem(m - k + mp, mp)
+        both = jnp.concatenate([gall[0, m], gall[1, m]], axis=0)
+        for j in range(nx):
+            xs[k, j] = dot_nn(sht[s, j * chunk : (j + 1) * chunk, :], both).astype(BF16)
+        if nx > 1:
+            start_x(k, (0, 1, 2, 3))
+
+    def pass_on(k):
+        if nx > 1:
+            x_copy(k, 0).wait_recv()
+            term = xs[k, right, :part, :].astype(F32) + xa[k, 0].astype(F32)
+            xs[k, right, :part, :] = term.astype(BF16)
+            start_x(k, (4,))
+            x_copy(k, 1).wait_recv()
+            term = xs[k, left, part:, :].astype(F32) + xa[k, 1].astype(F32)
+            xs[k, left, part:, :] = term.astype(BF16)
+            start_x(k, (5,))
+
+    def to_z(k):
+        total = xs[k, x].astype(F32)
+        if nx > 1:
+            for kind in (2, 3, 4, 5):
+                x_copy(k, kind).wait_recv()
+            total = total + xb[k, 0].astype(F32) + xb[k, 1].astype(F32)
+        yr[k] = total.astype(BF16)
+        scatter_z(k)
+
+    def z_target(k):
+        return 2 * lax.rem(m - k + mp, mp) + d
+
+    def z_copy(k, other):
+        e = 1 - d if other else d
+        rows = pl.ds(pl.multiple_of(e * part, part), part)
+        device = {"ctx": z_target(k) * nx + x}
+        if other:
+            device["dp"] = 1 - d
+        return remote(
+            yr.at[k, rows], zr.at[z], z_send.at[k, int(other)], z_recv.at[z], device
+        )
+
+    def scatter_z(k):
+        z_copy(k, True).start()
+        pending.append(z_copy(k, True).wait_send)
+
+        @pl.when(z_target(k) != z)
+        def _():
+            z_copy(k, False).start()
+
+        def finish():
+            @pl.when(z_target(k) != z)
+            def _():
+                z_copy(k, False).wait_send()
+
+        pending.append(finish)
+
+        @pl.when(z_target(k) == z)
+        def _():
+            zr[z] = yr[k, pl.ds(pl.multiple_of(d * part, part), part), :]
+
+    for i, k in enumerate(order):
+        partial_terms(k)
+        if i >= 1:
+            pass_on(order[i - 1])
+        if i >= 2:
+            to_z(order[i - 2])
+    pass_on(order[-1])
+    for k in near_first:
+        g_copies[k].wait_recv()
+        to_partner(k).start()
+        pending.append(to_partner(k).wait_send)
+    if mp > 1:
+        to_z(order[-2])
+    for k in near_first:
         to_partner(k).wait_recv()
-        for j in range(nx):
-            rows = slice(j * chunk, (j + 1) * chunk)
-            xs[k, j] = (
-                dot_nn(sht[rows, :tokens], gall[0, h]) + dot_nn(sht[rows, tokens:], gall[1, h])
-            ).astype(BF16)
-        for kx in range(1, nx):
-            x_copy(k, kx).start()
-
     ig = dot_nt(gall[1 - d, 0], wh[0])
     for h in range(1, mp):
         ig = ig + dot_nt(gall[1 - d, h], wh[h])
@@ -495,51 +616,7 @@
     for h in range(1, mp):
         ig = ig + dot_nt(gall[d, h], wh[h])
     image_out[:, pl.ds(pl.multiple_of(d * half, half), half)] = ig.astype(BF16)
-
-    def y_copy(k):
-        return remote(
-            ys.at[k], yr.at[k], y_send.at[k], y_recv.at[k], {"mp": lax.rem(m - k + mp, mp)}
-        )
-
-    def z_target(k):
-        return 2 * lax.rem(m + k, mp) + d
-
-    def z_copy(k, other):
-        e = 1 - d if other else d
-        rows = pl.ds(pl.multiple_of(e * part, part), part)
-        device = {"ctx": z_target(k) * nx + x}
-        if other:
-            device["dp"] = 1 - d
-        return remote(
-            yr.at[k, rows], zr.at[z], z_send.at[k, int(other)], z_recv.at[z], device
-        )
-
-    def scatter_z(k):
-        z_copy(k, True).start()
-
-        @pl.when(z_target(k) != z)
-        def _():
-            z_copy(k, False).start()
-
-        @pl.when(z_target(k) == z)
-        def _():
-            zr[z] = yr[k, pl.ds(pl.multiple_of(d * part, part), part), :]
-
-    for k in order:
-        total = xs[k, x].astype(F32)
-        for kx in range(1, nx):
-            x_copy(k, kx).wait_recv()
-            total = total + xr[k, kx].astype(F32)
-        if k:
-            ys[k] = total.astype(BF16)
-            y_copy(k).start()
-        else:
-            yr[0] = total.astype(BF16)
-            scatter_z(0)
-    for k in order:
-        if k:
-            y_copy(k).wait_recv()
-            scatter_z(k)
+    to_z(order[-1])
 
     ig_copy.wait()
     image_out[:, pl.ds(pl.multiple_of((1 - d) * half, half), half)] = ig_recv[...]
@@ -564,24 +641,8 @@
     wg_copy.wait()
     weight_out[pl.ds(pl.multiple_of((1 - d) * part, part), part), :] = wg_recv[...]
 
-    for k in order:
-        p_copies[k].wait_send()
-        to_partner(k).wait_send()
-        for kx in range(1, nx):
-            x_copy(k, kx).wait_send()
-        if k:
-            for group in (wa, wb, wc, i_copies, g_copies):
-                group[k].wait_send()
-            y_copy(k).wait_send()
-            for kx in range(1, nx):
-                fx_copy(k, kx).wait_send()
-            each_z(k, lambda copy: copy.wait_send())
-        z_copy(k, True).wait_send()
-
-        @pl.when(z_target(k) != z)
-        def _(k=k):
-            z_copy(k, False).wait_send()
-    put_out.wait()
+    for finish in pending:
+        finish()
 
 
 def fused(place, docs, text, states, weights, queries, grads, n, mp):
@@ -596,7 +657,7 @@
     nz = 2 * mp
     chunk = half // nx
     vmem = pl.BlockSpec(memory_space=pltpu.VMEM)
-    hbm = pl.BlockSpec(memory_space=pl.ANY)
+    hbm = pl.BlockSpec(memory_space=pltpu.HBM)
     dma = pltpu.SemaphoreType.DMA
     low = lambda *shape: pltpu.VMEM(shape, BF16)
     wide = lambda *shape: pltpu.VMEM(shape, F32)
@@ -608,11 +669,11 @@
             jax.ShapeDtypeStruct((chunk, width), F32),
         ),
         in_specs=[vmem, vmem, hbm, hbm, hbm, hbm, hbm],
-        out_specs=(hbm, vmem, vmem),
+        out_specs=(pl.BlockSpec(memory_space=pl.ANY), vmem, vmem),
         scratch_shapes=[
             low(2, tokens, half),
             low(mp, half, width),
-            low(half, 2 * tokens),
+            low(mp, half, 2 * tokens),
             wide(mp, tokens, width),
             wide(mp, tokens, width),
             wide(mp, tokens, width),
@@ -640,15 +701,17 @@
             low(2 * size, hd),
             low(2 * size, hd),
             low(hd, 2 * size),
-            wide(2 * size, hd),
-            wide(2 * size, hd),
+            low(2, heads_width // hd * block, hd),
+            low(2, heads_width // hd * block, hd),
+            low(2, size + block, heads_width // hd * block),
+            low(2, size + block, heads_width // hd * block),
             low(tokens, width),
             low(tokens, width),
             low(slots, width),
             low(2, mp, tokens, width),
             low(mp, nx, chunk, width),
-            low(mp, nx, chunk, width),
-            low(mp, chunk, width),
+            low(mp, 2, chunk // 2, width),
+            low(mp, 2, chunk, width),
             low(mp, chunk, width),
             low(nz, chunk // 2, width),
             wide(chunk // 2, width),
@@ -665,17 +728,24 @@
             dma((6,)),
             *[dma((n,))] * 2,
             *[dma((mp,))] * 4,
-            *[dma((mp, nx))] * 2,
+            *[dma((mp, 6))] * 2,
             *[dma((mp,))] * 2,
             dma((mp, 2)),
             dma((nz,)),
             dma((4,)),
         ],
         compiler_params=pltpu.CompilerParams(
-            collective_id=0, has_side_effects=True, vmem_limit_bytes=62 << 20
+            collective_id=0, has_side_effects=True, vmem_limit_bytes=47 << 20
         ),
         name="fused",
-    )(place, docs, text, states, weights, queries, grads)
+    )(
+        place,
+        docs,
+        *(
+            pltpu.with_memory_space_constraint(a, pltpu.HBM)
+            for a in (text, states, weights, queries, grads)
+        ),
+    )
 
 
 def per_device(image_states, place_index, doc_ids, queries, text_kv, kv_weight, d_out):

time: 138 us -> 121 us (0.88)
  Pallas kernels: 132 us -> 116 us
    pallas_call x1, Pallas kernels: 132 us -> 116 us  [fused(): pl.pallas_call(functools.partial(fused_kernel, n, mp, nx, nz, hd), out_sh...]
    unnamed x5 -> x7, local copies, waits for them, and re-layouts: 5.31 us -> 4.23 us
where the time goes in v3:
time: 121 us
  Pallas kernels  116 us (96%)
  local copies, waits for them, and re-layouts  4.23 us (3%)
    pallas_call x1, Pallas kernels, fused(): pl.pallas_call(functools.partial(fused_kernel, n, mp, nx, nz, hd), out_sh...  116 us
    unnamed x7, local copies, waits for them, and re-layouts  4.23 us

profile of v3, /device:TPU:17, one launch (start us, length us, event | category | flops | bytes accessed | tf_op | source)
XLA Modules:
  0.0 121.0 jit_solution(15984545664539507909)
XLA Ops:
  0.6 0.0 copy-start
  0.6 0.8 copy-done
  1.5 0.0 copy-start.1
  1.5 0.8 copy-done.1
  2.2 116.1 %fused.1 = (bf16[512,1024]{1,0:T(8,128)(2,1)S(1)}, bf16[256,2048]{1,0:T(8,128)(2,1)S(1)}, f32[256,256]{1,0:T(8,128)S(1)}) custom-call(s32[1,8192]{1,0:T(1,128)S(1)} %copy-done.1, s32[1,16384]{1,0:T(1,128)S(1)} %copy-done, bf16[512,256]{1,0:T(8,128)(2,1)} %bitcast.15, bf16[256,2048]{1,0:T(8,128)(2,1)} %bitcast.12, bf16[8192,256]{1,0:T(8,128)(2,1)} %bitcast.11, ...), custom_call_target="tpu_custom_call" | custom-call | tf_op jit(solution)/shard_map/fused/pallas_call | solution.py:664
  118.4 1.0 copy.13
  119.3 1.0 copy.14
  120.3 0.7 copy.15
Async XLA Ops:
  0.6 0.8 copy-start
  1.5 0.8 copy-start.1
